TPU v7x, 32 devices: a whole 2x2x4 slice. The times are simulated.
32 devices in a mesh: dp: 16 (over z, y, x), tensor: 2 (over core).
Axes of the slice: x: 2, y: 2, z: 4, core: 2. Of those that a mesh axis runs over, the one named last changes fastest.
Arguments:
- tokens: bfloat16 [8192, 1024], P('dp', 'tensor'), may hold values from -6 to 6
- norm_gains: float32 [2, 1024], replicated, may hold values from 0.5 to 1.5
- qkv_weight: bfloat16 [1024, 3, 1024], P(None, None, 'tensor'), may hold values from -0.1875 to 0.1875
- conv_weight: float32 [4, 3, 1024], P(None, None, 'tensor'), may hold values from -2 to 2
- log_decay: float32 [16, 8, 512], P('dp', 'tensor'), may hold values from -1 to 0
- regular: float32 [8, 128], P('tensor'), may hold values from 0.25 to 1
- out_weight: bfloat16 [1024, 1024], P('tensor'), may hold values from -0.1875 to 0.1875
- gate_up_weight: bfloat16 [1024, 2, 1536], P(None, None, 'tensor'), may hold values from -0.1875 to 0.1875
- down_weight: bfloat16 [1536, 1024], P('tensor'), may hold values from -0.15625 to 0.15625
- prefix_cache: float32 [16, 8, 2, 128, 128], P('dp', 'tensor'), as said below
- prefix_tail: float32 [16, 3, 3, 1024], P('dp', None, None, 'tensor'), may hold values from -6 to 6
- suffix_len: int32 [16], P('dp'), may hold values from 1 to 512, as said below
- request_group: int32 [16], P('dp'), may hold values from 0 to 3
- prefix_owner: int32 [4], replicated, may hold values from 0 to 15, as said below
Outputs:
- mixed: bfloat16 [8192, 1024], P('dp', 'tensor')
- final_state: float32 [16, 8, 2, 128, 128], P('dp', 'tensor')
- final_tail: float32 [16, 3, 3, 1024], P('dp', None, None, 'tensor')
Inputs may be any that keep to these rules, and one draw needn't show every extreme that they name: `suffix_len`: every request has 1 to 512 live rows; in every draw one request has exactly 512. `prefix_owner`: the owners of the groups are distinct slots. prefix_cache[s, h, 0] is symmetric positive definite.
All inputs are finite; a program needn't handle non-finite values.
Results may differ from a plain program's by a relative error of at most 0.0067.
Values may be sent and summed in bfloat16 or wider, within the bound.
No kernel may reach another device: no remote copies, remote signals or barrier semaphores. Data moves between devices by JAX's collectives and lax.ppermute only.
A program may use at most 128 MiB of HBM per device.

v0:
```python
import jax
import jax.numpy as jnp
from jax import lax
from jax.sharding import PartitionSpec as P

DK = 128
CONV = 4
BLOCK = 128
ITERS = 4


PRECISE = lax.Precision.HIGHEST


def rms_rows(values_in, gain):
    floats = values_in.astype(jnp.float32)
    inverse = lax.rsqrt(jnp.mean(floats * floats, axis=-1, keepdims=True) + 1e-05)
    return (floats * inverse * gain).astype(jnp.bfloat16)


def head_view(stacked):
    return stacked.reshape(stacked.shape[0], -1, DK).transpose(1, 0, 2)


def unit_heads(stacked):
    shaped = head_view(stacked)
    return shaped * lax.rsqrt(jnp.sum(shaped * shaped, axis=-1, keepdims=True) + 1e-06)


def mesa_block(queries, key_rows, value_rows, log_gate, hstate, gstate, regular):
    cumulative = jnp.cumsum(log_gate, axis=1)
    rows_count = log_gate.shape[1]
    causal_mask = jnp.arange(rows_count)[:, None] >= jnp.arange(rows_count)[None, :]
    differ = cumulative[:, :, None] - cumulative[:, None, :]
    weights = jnp.where(causal_mask[None], jnp.exp(jnp.minimum(differ, 0.0)), 0.0)
    growth = jnp.exp(cumulative)[:, :, None]
    solved = jnp.zeros_like(queries)
    residual = queries
    search = queries
    norm_now = jnp.sum(residual * residual, axis=-1, keepdims=True)
    for iteration in range(ITERS):
        through = jnp.einsum("hcd,hde->hce", search, hstate, precision=PRECISE)
        apply_correlation = (
            jnp.einsum("hcd,hid->hci", search, key_rows, precision=PRECISE) * weights
        )
        local_part = jnp.einsum("hci,hid->hcd", apply_correlation, key_rows, precision=PRECISE)
        applied = growth * through + local_part + regular[:, None, :] * search
        step_size = norm_now / jnp.sum(search * applied, axis=-1, keepdims=True)
        solved = solved + step_size * search
        residual = residual - step_size * applied
        norm_next = jnp.sum(residual * residual, axis=-1, keepdims=True)
        search = residual + norm_next / norm_now * search
        norm_now = norm_next
    recall = jnp.einsum("hcd,hed->hce", solved, gstate, precision=PRECISE)
    correlation = jnp.einsum("hcd,hid->hci", solved, key_rows, precision=PRECISE) * weights
    output = growth * recall + jnp.einsum(
        "hci,hie->hce", correlation, value_rows, precision=PRECISE
    )
    decay_tail = jnp.exp(cumulative[:, -1:] - cumulative)[:, :, None]
    decay_last = jnp.exp(cumulative[:, -1])[:, None, None]
    hstate_new = decay_last * hstate + jnp.einsum(
        "hid,hie->hde", key_rows * decay_tail, key_rows, precision=PRECISE
    )
    gstate_new = decay_last * gstate + jnp.einsum(
        "hie,hid->hed", value_rows * decay_tail, key_rows, precision=PRECISE
    )
    return (output, hstate_new, gstate_new)


def mixer(projected, conv_weight, tail_rows, log_gate, regular, state_pair, length, block_limit):
    rows_total = projected.shape[0]
    shaped = projected.reshape(rows_total, 3, -1)
    extended = jnp.concatenate([tail_rows, shaped], axis=0)
    convolved = conv_weight[0] * extended[0:rows_total]
    for tap_index in range(1, CONV):
        convolved = (
            convolved + conv_weight[tap_index] * extended[tap_index : tap_index + rows_total]
        )
    activated = jax.nn.silu(convolved)
    new_tail = lax.dynamic_slice_in_dim(extended, length, CONV - 1, 0)
    live_rows = jnp.arange(rows_total) < length
    queries = unit_heads(activated[:, 0])
    key_rows = jnp.where(live_rows[None, :, None], unit_heads(activated[:, 1]), 0.0)
    value_rows = jnp.where(live_rows[None, :, None], head_view(activated[:, 2]), 0.0)
    gate_logs = jnp.where(live_rows[None, :], log_gate, 0.0)

    def block_step(block_id, loop_state):
        hstate, gstate, heads_out = loop_state
        start_row = (block_id * BLOCK).astype(jnp.int32)

        def take_block(array_in):
            return lax.dynamic_slice_in_dim(array_in, start_row, BLOCK, 1)

        out_block, hstate, gstate = mesa_block(
            take_block(queries),
            take_block(key_rows),
            take_block(value_rows),
            take_block(gate_logs),
            hstate,
            gstate,
            regular,
        )
        heads_out = lax.dynamic_update_slice_in_dim(heads_out, out_block, start_row, 1)
        return (hstate, gstate, heads_out)

    hstate, gstate, heads_out = lax.fori_loop(
        0, block_limit, block_step, (state_pair[:, 0], state_pair[:, 1], jnp.zeros_like(queries))
    )
    heads_flat = heads_out.transpose(1, 0, 2).reshape(rows_total, -1).astype(jnp.bfloat16)
    return (heads_flat, jnp.stack([hstate, gstate], axis=1), new_tail)


def project(rows_in, gain, weight):
    whole_rows = lax.all_gather(rows_in, "tensor", axis=1, tiled=True)
    return jnp.dot(rms_rows(whole_rows, gain), weight, preferred_element_type=jnp.float32)


def reduce_features(partial_rows):
    return lax.psum_scatter(partial_rows, "tensor", scatter_dimension=1, tiled=True)


def on_device(
    tokens,
    norm_gains,
    qkv_weight,
    conv_weight,
    log_decay,
    regular,
    out_weight,
    gate_up_weight,
    down_weight,
    prefix_cache,
    prefix_tail,
    suffix_len,
    request_group,
    prefix_owner,
):
    length = suffix_len[0]
    group_id = request_group[0]
    rows_total = tokens.shape[0]
    owned = (prefix_owner == lax.axis_index("dp")).astype(jnp.float32)
    cache_terms = owned[:, None, None, None, None] * prefix_cache
    tail_terms = owned[:, None, None, None] * prefix_tail
    cache_all, tail_all = lax.psum((cache_terms, tail_terms), "dp")
    chosen = (jnp.arange(cache_all.shape[0]) == group_id).astype(jnp.float32)
    state_pair = jnp.sum(chosen[:, None, None, None, None] * cache_all, axis=0)
    tail_rows = jnp.sum(chosen[:, None, None, None] * tail_all, axis=0)
    block_limit = rows_total // BLOCK
    projected = project(tokens, norm_gains[0], qkv_weight.reshape(qkv_weight.shape[0], -1))
    heads_flat, state_out, tail_out = mixer(
        projected, conv_weight, tail_rows, log_decay[0], regular, state_pair, length, block_limit
    )
    attended = reduce_features(jnp.dot(heads_flat, out_weight, preferred_element_type=jnp.float32))
    middle = (tokens.astype(jnp.float32) + attended).astype(jnp.bfloat16)
    gate_up = project(
        middle, norm_gains[1], gate_up_weight.reshape(gate_up_weight.shape[0], -1)
    ).reshape(rows_total, 2, -1)
    hidden = (jax.nn.silu(gate_up[:, 0]) * gate_up[:, 1]).astype(jnp.bfloat16)
    forward = reduce_features(jnp.dot(hidden, down_weight, preferred_element_type=jnp.float32))
    live_rows = jnp.arange(rows_total) < length
    result = jnp.where(live_rows[:, None], middle.astype(jnp.float32) + forward, 0.0).astype(
        jnp.bfloat16
    )
    return (result, state_out[None], tail_out[None])


def solution(mesh):
    return jax.shard_map(
        on_device,
        mesh=mesh,
        in_specs=(
            P("dp", "tensor"),
            P(),
            P(None, None, "tensor"),
            P(None, None, "tensor"),
            P("dp", "tensor", None),
            P("tensor", None),
            P("tensor", None),
            P(None, None, "tensor"),
            P("tensor", None),
            P("dp", "tensor", None, None, None),
            P("dp", None, None, "tensor"),
            P("dp"),
            P("dp"),
            P(),
        ),
        out_specs=(
            P("dp", "tensor"),
            P("dp", "tensor", None, None, None),
            P("dp", None, None, "tensor"),
        ),
        check_vma=False,
    )
```

profile of v0, /device:TPU:0, one launch (start us, length us, event | category | flops | bytes accessed | tf_op | source)
XLA Modules:
  0.0 302.5 jit_solution(3747054038898896403)
XLA Ops:
  10.9 2.7 broadcast_multiply_fusion
  15.1 4.7 %copy.83 = bf16[1024,3,512]{0,2,1:T(8,128)(2,1)} copy(bf16[1024,3,512]{2,0,1:T(8,128)(2,1)} %param.18) | data formatting | bytes 6291456 | tf_op args[2]
  19.9 2.3 all-gather.3.cloned.1.call-done
  23.7 5.9 %fusion.47 = f32[512,3,512]{0,2,1:T(8,128)} fusion(bf16[1024,3,512]{0,2,1:T(8,128)(2,1)} %copy.83, bf16[512,1024]{1,0:T(8,128)(2,1)} %all-gather.3.cloned.1.call-done, f32[1024]{0:T(1024)S(1)} %bitcast.153, f32[512]{0:T(512)S(1)} %add_rsqrt_fusion.3), kind=kOutput, calls=%fused_computation.92 | convolution fusion | flops 1612709888 | bytes 7346176 | tf_op jit(solution)/shard_map/dot_general | solution.py:115
  29.5 117.2 %all-reduce.3.cloned.1.call-done = (f32[4,4,2,128,128]{4,3,2,1,0:T(8,128)}, f32[4,3,3,512]{3,0,2,1:T(4,128)}) async-done(((f32[4,4,2,128,128]{4,3,2,1,0:T(8,128)}, f32[4,3,3,512]{3,0,2,1:T(4,128)}), (f32[4,4,2,128,128]{4,3,2,1,0:T(8,128)}, f32[4,3,3,512]{3,0,2,1:T(4,128)})) %all-reduce.3.cloned.1.call-update) | async-done | bytes 2170896 | tf_op jit(solution)/shard_map/psum | solution.py:144
  146.7 1.9 multiply_reduce_fusion.7
  150.0 9.2 %divide_multiply_fusion = f32[512,3,512]{0,2,1:T(8,128)S(1)} fusion(f32[512,3,512]{0,2,1:T(8,128)} %fusion.47, f32[3,3,512]{0,2,1:T(8,128)S(1)} %copy.84, f32[3,512]{1,0:T(4,128)S(1)} %get-tuple-element.212, f32[3,512]{1,0:T(4,128)S(1)} %get-tuple-element.213, f32[3,512]{1,0:T(4,128)S(1)} %get-tuple-element.214, f32[3,512]{1,0:T(4,128)S(1)} %get-tuple-element.215), kind=kLoop, calls=%fused_computation.94 | loop fusion | flops 11010048 | bytes 6334464 | tf_op jit(solution)/shard_map/jit(silu)/mul | solution.py:79
  159.2 1.8 fusion.75
  162.5 2.6 copy.86
  165.1 2.4 select_bitcast_fusion
  174.2 74.5 %while.17 = (s32[]{:T(128)}, f32[4,128,128]{2,1,0:T(8,128)S(1)}, f32[4,128,128]{2,1,0:T(8,128)S(1)}, bf16[4,512,128]{1,2,0:T(8,128)(2,1)}, f32[4,512]{1,0:T(4,12...) while((s32[]{:T(128)}, f32[4,128,128]{2,1,0:T(8,128)S(1)}, ...), condition=%wide.region_17.18_spmd, body=%wide.region_7.17_spmd.sunk | while | flops 1716731392 | bytes 26850652 | solution.py:106
  189.8 1.7 convolution_add_fusion.11
  208.4 1.7 convolution_add_fusion.11
  248.8 3.5 %fusion.78 = f32[512,1024]{1,0:T(8,128)} fusion(bf16[512,512]{0,1:T(8,128)(2,1)} %bitcast.149, bf16[512,1024]{1,0:T(8,128)(2,1)} %param.22), kind=kOutput, calls=%fused_computation.154 | convolution fusion | flops 536870912 | bytes 3670016 | tf_op jit(solution)/shard_map/dot_general | solution.py:153
  252.4 9.1 %reduce-scatter.3.cloned.1.call-done = f32[512,512]{1,0:T(8,128)} async-done(((f32[512,1024]{1,0:T(8,128)}), f32[512,512]{1,0:T(8,128)}) %reduce-scatter.3.cloned.1.call-update) | async-done | bytes 1048592 | tf_op jit(solution)/shard_map/reduce_scatter | solution.py:119
  261.5 2.2 add_convert_fusion
  263.7 4.2 %copy.125 = bf16[128,8,2,768]{3,1,2,0:T(8,128)(2,1)} copy(bf16[128,8,2,768]{3,2,1,0:T(2,128)(2,1)} %bitcast.147) | data formatting | bytes 6291456
  267.9 4.7 %copy.89 = bf16[1536,1024]{1,0:T(8,128)(2,1)} copy(bf16[1536,1024]{0,1:T(8,128)(2,1)} %bitcast.143) | data formatting | bytes 6291456 | tf_op jit(solution)/shard_map/dot_general | solution.py:115
  275.6 4.1 %fusion.58 = f32[512,2,768]{2,0,1:T(8,128)S(1)} fusion(bf16[2,768,1024]{2,1,0:T(8,128)(2,1)} %bitcast.148, bf16[512,1024]{1,0:T(8,128)(2,1)} %all-gather.5.cloned.1.call-done, f32[1024]{0:T(1024)S(1)} %bitcast.152, f32[512]{0:T(512)S(1)} %add_rsqrt_fusion.2), kind=kOutput, calls=%fused_computation.111 | convolution fusion | flops 1612709888 | bytes 7346176 | tf_op jit(solution)/shard_map/dot_general | solution.py:115
  279.8 2.4 fusion.71
  282.2 2.8 fusion.70
  285.1 2.0 copy.91
  287.9 5.3 %reduce-scatter.5.cloned.1.call-done = f32[512,512]{1,0:T(8,128)} async-done(((f32[512,1024]{1,0:T(8,128)}), f32[512,512]{1,0:T(8,128)}) %reduce-scatter.5.cloned.1.call-update) | async-done | bytes 1048592 | tf_op jit(solution)/shard_map/reduce_scatter | solution.py:119
  293.2 2.2 select_convert_fusion
  (220 shorter events, 88.5 us)
Async XLA Ops:
  8.0 271.8 %copy-start = (bf16[768,1024]{1,0:T(8,128)(2,1)S(1)}, bf16[768,1024]{1,0:T(8,128)(2,1)}, u32[]{:S(2)}) copy-start(bf16[768,1024]{1,0:T(8,128)(2,1)} %param.24) | copy-start | bytes 4718596
  8.0 14.1 %all-gather.3.cloned.1.call-start = ((), (), s32[]{:S(2)}) async-start(), calls=%async_computation.2 | async-start | bytes 1572864 | tf_op jit(solution)/shard_map/all_gather | solution.py:114
  8.7 138.0 %all-reduce.3.cloned.1.call-start = ((), (), s32[]{:S(2)}) async-start(), calls=%async_computation.6 | async-start | bytes 4341760 | tf_op jit(solution)/shard_map/psum | solution.py:144
  13.7 247.8 %reduce-scatter.3.cloned.1.call-start = ((), (), s32[]{:S(2)}) async-start(), calls=%async_computation.3 | async-start | bytes 3145728 | tf_op jit(solution)/shard_map/reduce_scatter | solution.py:119
  15.0 4.7 %copy-start.9 = (f32[2,1024]{1,0:T(2,128)S(1)}, f32[2,1024]{1,0:T(2,128)}, u32[]{:S(2)}) copy-start(f32[2,1024]{1,0:T(2,128)} %param.17) | copy-start | bytes 24580
  15.0 4.8 %copy-start.10 = (f32[1,4,512]{2,1,0:T(4,128)S(1)}, f32[1,4,512]{2,1,0:T(4,128)}, u32[]{:S(2)}) copy-start(f32[1,4,512]{2,1,0:T(4,128)} %param.20) | copy-start | bytes 24580
  15.1 4.8 %copy-start.8 = (f32[4,3,512]{2,0,1:T(4,128)S(1)}, f32[4,3,512]{2,0,1:T(4,128)}, u32[]{:S(2)}) copy-start(f32[4,3,512]{2,0,1:T(4,128)} %param.19) | copy-start | bytes 73732
  150.0 9.2 %copy-start.3 = (f32[3,3,512]{0,2,1:T(8,128)}, f32[3,3,512]{0,2,1:T(8,128)S(1)}, u32[]{:S(2)}) copy-start(f32[3,3,512]{0,2,1:T(8,128)S(1)} %copy.84) | copy-start | bytes 55300
  169.2 5.0 %copy-start.7 = (f32[4,128]{1,0:T(4,128)S(1)}, f32[4,128]{1,0:T(4,128)}, u32[]{:S(2)}) copy-start(f32[4,128]{1,0:T(4,128)} %param.21) | copy-start | bytes 6148
  170.8 1.0 copy-start.2
  174.5 6.1 %copy-start.1 = (f32[4,512,128]{2,1,0:T(8,128)S(1)}, f32[4,512,128]{2,1,0:T(8,128)}, u32[]{:S(2)}) copy-start(f32[4,512,128]{2,1,0:T(8,128)} %get-tuple-element.332) | copy-start | bytes 3145732 | tf_op jit(solution)/shard_map/while
  193.2 6.1 %copy-start.1 = (f32[4,512,128]{2,1,0:T(8,128)S(1)}, f32[4,512,128]{2,1,0:T(8,128)}, u32[]{:S(2)}) copy-start(f32[4,512,128]{2,1,0:T(8,128)} %get-tuple-element.332) | copy-start | bytes 3145732 | tf_op jit(solution)/shard_map/while
  211.8 6.1 %copy-start.1 = (f32[4,512,128]{2,1,0:T(8,128)S(1)}, f32[4,512,128]{2,1,0:T(8,128)}, u32[]{:S(2)}) copy-start(f32[4,512,128]{2,1,0:T(8,128)} %get-tuple-element.332) | copy-start | bytes 3145732 | tf_op jit(solution)/shard_map/while
  230.5 6.1 %copy-start.1 = (f32[4,512,128]{2,1,0:T(8,128)S(1)}, f32[4,512,128]{2,1,0:T(8,128)}, u32[]{:S(2)}) copy-start(f32[4,512,128]{2,1,0:T(8,128)} %get-tuple-element.332) | copy-start | bytes 3145732 | tf_op jit(solution)/shard_map/while
  248.8 12.7 %copy-start.6 = (bf16[512,512]{1,0:T(8,128)(2,1)S(1)}, bf16[512,512]{1,0:T(8,128)(2,1)}, u32[]{:S(2)}) copy-start(bf16[512,512]{1,0:T(8,128)(2,1)} %param.16) | copy-start | bytes 1572868
  252.3 21.8 %all-gather.5.cloned.1.call-start = ((), (), s32[]{:S(2)}) async-start(), calls=%async_computation.4 | async-start | bytes 1572864 | tf_op jit(solution)/shard_map/all_gather | solution.py:114
  263.7 29.5 %reduce-scatter.5.cloned.1.call-start = ((), (), s32[]{:S(2)}) async-start(), calls=%async_computation.5 | async-start | bytes 3145728 | tf_op jit(solution)/shard_map/reduce_scatter | solution.py:119
  279.8 2.5 copy-start.4
  282.2 10.9 %copy-start.5 = (bf16[512,512]{1,0:T(8,128)(2,1)S(1)}, bf16[512,512]{1,0:T(8,128)(2,1)}, u32[]{:S(2)}) copy-start(bf16[512,512]{1,0:T(8,128)(2,1)} %add_convert_fusion) | copy-start | bytes 1572868
Sparse Core Ops, SparseCore 0:
  10.4 11.7 all-gather.2
  252.5 8.9 reduce-scatter.2
  263.8 10.2 all-gather.4
  282.3 10.7 reduce-scatter.4
Sparse Core Ops, SparseCore 1:
  15.6 131.1 all-reduce.2
where the time goes:
time: 304 us; the launch traced here: 302 us
  waiting for transfers between devices  136 us (45%)
  matrix products  73.7 us (24%)
  other arithmetic  45.3 us (15%)
  local copies, waits for them, and re-layouts  29.7 us (10%)
  between operations  16.7 us (5%)
    psum x1, waiting for transfers between devices, on_device(): cache_all, tail_all = lax.psum((cache_terms, tail_terms), 'dp')  117 us
    dot_general x16, matrix products, mesa_block(): jnp.einsum('hcd,hid->hci', search, key_rows, precision=PRECISE) * weights  14.7 us
    reduce_scatter x2, waiting for transfers between devices, reduce_features(): lax.psum_scatter(partial_rows, 'tensor', scatter_dimension=1, tiled=True)  14.3 us
    dot_general x16, matrix products, mesa_block(): jnp.einsum('hci,hid->hcd', apply_correlation, key_rows, precision=PRECISE)  12.5 us
    unnamed x26, local copies, waits for them, and re-layouts  12.3 us
    dot_general x16, matrix products, mesa_block(): through = jnp.einsum('hcd,hde->hce', search, hstate, precision=PRECISE)  10.1 us
    dot_general x2, matrix products, project(): jnp.dot(rms_rows(whole_rows, gain), weight, preferred_element_type=jnp.fl...  10 us
    mul x1, other arithmetic, mixer(): activated = jax.nn.silu(convolved)  9.18 us
  transfers between devices with their start and end apart: 5, of which 5 were waited for; matrix products, arithmetic and copies ran while one was open for 10% of the time, Pallas kernels for 0%

commit v1 on v0

v1 whole, which is shorter than its diff:
```python
import functools

import jax
import jax.numpy as jnp
from jax import lax
from jax.experimental import pallas as pl
from jax.experimental.pallas import tpu as pltpu
from jax.sharding import PartitionSpec as P

DK = 128
CONV = 4
BLOCK = 128
ITERS = 4
LANES = 128
BF16 = jnp.bfloat16
F32 = jnp.float32


def rms_rows(floats, gain):
    inverse = lax.rsqrt(jnp.mean(floats * floats, axis=-1, keepdims=True) + 1e-05)
    return (floats * inverse * gain).astype(BF16)


def other_core(array_in):
    return lax.ppermute(array_in, "tensor", [(0, 1), (1, 0)])


def halves(value):
    high = value.astype(BF16)
    return high, (value - high.astype(F32)).astype(BF16)


def dot_nn(left, right):
    return lax.dot_general(left, right, (((1,), (0,)), ((), ())), preferred_element_type=F32)


def dot_nt(left, right):
    return lax.dot_general(left, right, (((1,), (1,)), ((), ())), preferred_element_type=F32)


def dot_tn(left, right):
    return lax.dot_general(left, right, (((0,), (0,)), ((), ())), preferred_element_type=F32)


def pack_kernel(group, cache, tail, packed):
    count, rows, _ = packed.shape
    heads = cache.shape[0]
    share = count // heads
    state_rows = rows - 8
    tail_rows = -(-(CONV - 1) * 3 // share)
    tag = jnp.full((1, LANES), group[0], jnp.int32).astype(F32)
    for head in range(heads):
        lanes = slice(head * DK, (head + 1) * DK)
        for piece in range(share):
            plane, offset = divmod(piece * state_rows, DK)
            parts = [cache[head, plane, offset : offset + state_rows, :]]
            for index in range(piece * tail_rows, (piece + 1) * tail_rows):
                if index < (CONV - 1) * 3:
                    parts.append(tail[index // 3, index % 3 : index % 3 + 1, lanes])
                else:
                    parts.append(tag)
            parts.append(jnp.broadcast_to(tag, (8 - tail_rows, LANES)))
            packed[head * share + piece] = jnp.concatenate(parts, axis=0).astype(BF16)


def pack(prefix_cache, prefix_tail, request_group, count):
    rows = prefix_cache.shape[0] * 2 * DK // count + 8
    return pl.pallas_call(
        pack_kernel,
        out_shape=jax.ShapeDtypeStruct((count, rows, LANES), BF16),
        in_specs=[
            pl.BlockSpec(memory_space=pltpu.SMEM),
            pl.BlockSpec(memory_space=pltpu.VMEM),
            pl.BlockSpec(memory_space=pltpu.VMEM),
        ],
        out_specs=pl.BlockSpec(memory_space=pltpu.VMEM),
        name="pack",
    )(request_group, prefix_cache, prefix_tail)


def route_kernel(owners, arrived, leaving):
    count, rows, _ = arrived.shape
    groups = owners.shape[0]
    held = [arrived[owners[group]].astype(F32) for group in range(groups)]

    def fill(slot, carry):
        wanted = arrived[slot].astype(F32)[rows - 1 : rows, :]
        chosen = held[0]
        for group in range(1, groups):
            chosen = jnp.where(wanted == float(group), held[group], chosen)
        leaving[slot] = chosen.astype(BF16)
        return carry

    lax.fori_loop(0, count, fill, 0)


def route(prefix_owner, arrived):
    return pl.pallas_call(
        route_kernel,
        out_shape=jax.ShapeDtypeStruct(arrived.shape, arrived.dtype),
        in_specs=[
            pl.BlockSpec(memory_space=pltpu.SMEM),
            pl.BlockSpec(memory_space=pltpu.VMEM),
        ],
        out_specs=pl.BlockSpec(memory_space=pltpu.VMEM),
        name="route",
    )(prefix_owner, arrived)


def mixer_kernel(
    length_ref,
    query_in,
    key_in,
    value_in,
    taps,
    prefix,
    decay,
    regular,
    out_weight,
    partial_out,
    state_out,
    tail_out,
    extended,
    total,
):
    rows_total = query_in.shape[1]
    blocks = rows_total // BLOCK
    head = pl.program_id(0)
    length = length_ref[0]
    share, chunk_rows, _ = prefix.shape
    state_rows = chunk_rows - 8
    tail_rows = -(-(CONV - 1) * 3 // share)
    chunks = [prefix[piece].astype(F32) for piece in range(share)]
    state = jnp.concatenate([chunk[:state_rows] for chunk in chunks], axis=0)
    hstate, gstate = state[:DK], state[DK:]

    live = lax.broadcasted_iota(jnp.int32, (rows_total, 1), 0) < length
    activated = []
    for part, source in enumerate((query_in, key_in, value_in)):
        for before in range(CONV - 1):
            piece, inside = divmod(before * 3 + part, tail_rows)
            place = state_rows + inside
            extended[5 + before : 6 + before, :] = chunks[piece][place : place + 1]
        extended[8 : 8 + rows_total, :] = source[0]
        convolved = taps[part, 0:1, :] * extended[pl.ds(5, rows_total), :]
        for tap in range(1, CONV):
            convolved = (
                convolved + taps[part, tap : tap + 1, :] * extended[pl.ds(5 + tap, rows_total), :]
            )
        tail_out[:, part, :] = extended[pl.ds(length + 5, CONV - 1), :]
        activated.append(convolved / (1.0 + jnp.exp(-convolved)))
    queries, key_rows, value_rows = activated
    queries = queries * lax.rsqrt(jnp.sum(queries * queries, axis=-1, keepdims=True) + 1e-06)
    key_rows = key_rows * lax.rsqrt(jnp.sum(key_rows * key_rows, axis=-1, keepdims=True) + 1e-06)
    key_rows = jnp.where(live, key_rows, 0.0)
    value_rows = jnp.where(live, value_rows, 0.0)

    lane = lax.broadcasted_iota(jnp.int32, (BLOCK, BLOCK), 1)
    row = lax.broadcasted_iota(jnp.int32, (BLOCK, BLOCK), 0)
    causal = row >= lane
    regular_row = regular[0]

    operands = []
    for block in range(blocks):
        rows = slice(block * BLOCK, (block + 1) * BLOCK)
        keys, values = key_rows[rows], value_rows[rows]
        gates = decay[0, :, block * BLOCK : (block + 1) * BLOCK]
        position = lax.broadcasted_iota(jnp.int32, (1, BLOCK), 1) + block * BLOCK
        gates = jnp.where(position < length, gates, 0.0)
        down = jnp.sum(jnp.where(causal, gates, 0.0), axis=1, keepdims=True)
        wide = jnp.broadcast_to(down, (BLOCK, BLOCK))
        differ = wide - wide.T
        weights = jnp.where(causal, jnp.exp(jnp.minimum(differ, 0.0)), 0.0)
        growth = jnp.exp(down)
        last = down[BLOCK - 1 : BLOCK, :]
        root_tail = jnp.exp(0.5 * (last - down))
        decay_last = jnp.exp(last)
        keys_high = keys.astype(BF16)
        operands.append(
            (
                keys_high,
                jnp.concatenate([hstate.astype(BF16), keys_high], axis=0),
                gstate.astype(BF16),
                values.astype(BF16),
                weights,
                growth,
            )
        )
        grown = jnp.concatenate([keys * root_tail, values * root_tail], axis=1).astype(BF16)
        update = dot_tn(grown, grown[:, :DK])
        hstate = decay_last * hstate + update[:DK]
        gstate = decay_last * gstate + update[DK:]
    state_out[0, 0] = hstate
    state_out[0, 1] = gstate

    search = [queries[block * BLOCK : (block + 1) * BLOCK] for block in range(blocks)]
    residual = list(search)
    solved = [None] * blocks
    correlated = [None] * blocks
    norm_now = [jnp.sum(r * r, axis=-1, keepdims=True) for r in residual]
    for iteration in range(ITERS):
        for block in range(blocks):
            k_high, mix_high, _, _, weights, growth = operands[block]
            p_now = search[block]
            p_high, p_low = halves(p_now)
            reach = (dot_nt(p_high, k_high) + dot_nt(p_low, k_high)) * weights
            b_high, b_low = halves(jnp.concatenate([growth * p_now, reach], axis=1))
            applied = dot_nn(b_high, mix_high) + dot_nn(b_low, mix_high) + regular_row * p_now
            step = norm_now[block] / jnp.sum(p_now * applied, axis=-1, keepdims=True)
            if iteration == 0:
                solved[block] = step * p_now
                correlated[block] = step * reach
            else:
                solved[block] = solved[block] + step * p_now
                correlated[block] = correlated[block] + step * reach
            if iteration < ITERS - 1:
                residual[block] = residual[block] - step * applied
                norm_next = jnp.sum(residual[block] * residual[block], axis=-1, keepdims=True)
                search[block] = residual[block] + norm_next / norm_now[block] * p_now
                norm_now[block] = norm_next
    outputs = []
    for block in range(blocks):
        _, _, g_high, v_high, _, growth = operands[block]
        recall = dot_nt((growth * solved[block]).astype(BF16), g_high)
        outputs.append(recall + dot_nn(correlated[block].astype(BF16), v_high))
    added = dot_nn(jnp.concatenate(outputs, axis=0).astype(BF16), out_weight[...])

    @pl.when(head == 0)
    def _():
        total[...] = added

    @pl.when((head > 0) & (head < pl.num_programs(0) - 1))
    def _():
        total[...] += added

    @pl.when(head == pl.num_programs(0) - 1)
    def _():
        partial_out[...] = (total[...] + added).astype(BF16)


def mixer(projected, taps, prefix, log_gate, regular, out_weight, length):
    rows_total = projected.shape[1]
    heads = regular.shape[0]
    width = heads * DK
    features = out_weight.shape[1]
    share = prefix.shape[0] // heads

    def columns(part):
        return pl.BlockSpec((1, rows_total, DK), lambda head: (part, 0, head))

    return pl.pallas_call(
        mixer_kernel,
        grid=(heads,),
        out_shape=(
            jax.ShapeDtypeStruct((rows_total, features), BF16),
            jax.ShapeDtypeStruct((heads, 2, DK, DK), F32),
            jax.ShapeDtypeStruct((CONV - 1, 3, width), F32),
        ),
        in_specs=[
            pl.BlockSpec(memory_space=pltpu.SMEM),
            columns(0),
            columns(1),
            columns(2),
            pl.BlockSpec((3, CONV, DK), lambda head: (0, 0, head)),
            pl.BlockSpec((share, prefix.shape[1], LANES), lambda head: (head, 0, 0)),
            pl.BlockSpec((1, 1, rows_total), lambda head: (head, 0, 0)),
            pl.BlockSpec((1, 1, DK), lambda head: (head, 0, 0)),
            pl.BlockSpec((DK, features), lambda head: (head, 0)),
        ],
        out_specs=(
            pl.BlockSpec((rows_total, features), lambda head: (0, 0)),
            pl.BlockSpec((1, 2, DK, DK), lambda head: (head, 0, 0, 0)),
            pl.BlockSpec((CONV - 1, 3, DK), lambda head: (0, 0, head)),
        ),
        scratch_shapes=[
            pltpu.VMEM((rows_total + 8, DK), F32),
            pltpu.VMEM((rows_total, features), F32),
        ],
        compiler_params=pltpu.CompilerParams(dimension_semantics=("arbitrary",)),
        name="mixer",
    )(
        length,
        projected,
        projected,
        projected,
        taps,
        prefix,
        log_gate[:, None, :],
        regular[:, None, :],
        out_weight,
    )


def feed_kernel(core, mine, theirs, partial, arrived, gain, gate, up, down, leaving, kept):
    half = mine.shape[1]
    features = 2 * half
    own = pl.multiple_of(core[0] * half, half)
    far = pl.multiple_of((1 - core[0]) * half, half)

    def middle(source, columns, rows):
        added = partial[rows, columns].astype(F32) + arrived[rows, columns].astype(F32)
        return (source[rows, :].astype(F32) + added).astype(BF16).astype(F32)

    step = 256
    for start in range(0, mine.shape[0], step):
        rows = slice(start, start + step)
        middle_own = middle(mine, pl.ds(own, half), rows)
        middle_far = middle(theirs, pl.ds(far, half), rows)
        squares = jnp.sum(
            middle_own * middle_own + middle_far * middle_far, axis=-1, keepdims=True
        )
        inverse = lax.rsqrt(squares * (1.0 / features) + 1e-05)
        normed_own = (middle_own * inverse * gain[:, pl.ds(own, half)]).astype(BF16)
        normed_far = (middle_far * inverse * gain[:, pl.ds(far, half)]).astype(BF16)

        def through(weight):
            return dot_nn(normed_own, weight[pl.ds(own, half), :]) + dot_nn(
                normed_far, weight[pl.ds(far, half), :]
            )

        gated = through(gate)
        hidden = (gated / (1.0 + jnp.exp(-gated)) * through(up)).astype(BF16)
        leaving[rows, :] = dot_nn(hidden, down[:, pl.ds(far, half)]).astype(BF16)
        kept[rows, :] = dot_nn(hidden, down[:, pl.ds(own, half)]) + middle_own


def feed(core, mine, theirs, partial, arrived, gain, gate, up, down):
    vmem = pl.BlockSpec(memory_space=pltpu.VMEM)
    return pl.pallas_call(
        feed_kernel,
        out_shape=(
            jax.ShapeDtypeStruct(mine.shape, BF16),
            jax.ShapeDtypeStruct(mine.shape, F32),
        ),
        in_specs=[pl.BlockSpec(memory_space=pltpu.SMEM)] + [vmem] * 8,
        out_specs=(vmem, vmem),
        name="feed",
    )(core, mine, theirs, partial, arrived, gain, gate, up, down)


def on_device(
    tokens,
    norm_gains,
    qkv_weight,
    conv_weight,
    log_decay,
    regular,
    out_weight,
    gate_up_weight,
    down_weight,
    prefix_cache,
    prefix_tail,
    suffix_len,
    request_group,
    prefix_owner,
):
    rows_total = tokens.shape[0]
    core = lax.axis_index("tensor")
    first = core == 0
    packed = pack(prefix_cache[0], prefix_tail[0], request_group, lax.axis_size("dp"))
    theirs = other_core(tokens)
    arrived = lax.all_to_all(packed, "dp", 0, 0)
    arrived, gate_weight, up_weight = lax.optimization_barrier(
        (arrived, gate_up_weight[:, 0, :], gate_up_weight[:, 1, :])
    )
    prefix = lax.all_to_all(route(prefix_owner, arrived), "dp", 0, 0)
    whole_rows = jnp.concatenate(
        [jnp.where(first, tokens, theirs), jnp.where(first, theirs, tokens)], axis=1
    ).astype(F32)
    normed = rms_rows(whole_rows, norm_gains[0])
    planes = jnp.transpose(qkv_weight, (1, 0, 2))
    projected = jnp.einsum("rd,jdc->jrc", normed, planes, preferred_element_type=F32)
    partial, state_out, tail_out = mixer(
        projected,
        jnp.transpose(conv_weight, (1, 0, 2)),
        prefix,
        log_decay[0],
        regular,
        out_weight,
        suffix_len,
    )
    leaving, kept = feed(
        core.reshape(1).astype(jnp.int32),
        tokens,
        theirs,
        partial,
        other_core(partial),
        norm_gains[1:2],
        gate_weight,
        up_weight,
        down_weight,
    )
    live_rows = jnp.arange(rows_total) < suffix_len[0]
    result = kept + other_core(leaving).astype(F32)
    result = jnp.where(live_rows[:, None], result, 0.0).astype(BF16)
    return (result, state_out[None], tail_out[None])


def solution(mesh):
    return jax.shard_map(
        on_device,
        mesh=mesh,
        in_specs=(
            P("dp", "tensor"),
            P(),
            P(None, None, "tensor"),
            P(None, None, "tensor"),
            P("dp", "tensor", None),
            P("tensor", None),
            P("tensor", None),
            P(None, None, "tensor"),
            P("tensor", None),
            P("dp", "tensor", None, None, None),
            P("dp", None, None, "tensor"),
            P("dp"),
            P("dp"),
            P(),
        ),
        out_specs=(
            P("dp", "tensor"),
            P("dp", "tensor", None, None, None),
            P("dp", None, None, "tensor"),
        ),
        check_vma=False,
    )
```

time: 304 us -> 85 us (0.28)
  waiting for transfers between devices: 136 us -> 10.4 us
  matrix products: 73.7 us -> 4.74 us
  other arithmetic: 45.3 us -> 3.63 us
  Pallas kernels: 0 us -> 27.9 us
  starting transfers between devices: 0.21 us -> 15.4 us
  between operations: 16.7 us -> 2.05 us
  local copies, waits for them, and re-layouts: 29.7 us -> 20.3 us
    psum x1 -> x0, waiting for transfers between devices: 117 us -> none  [on_device(): cache_all, tail_all = lax.psum((cache_terms, tail_terms), 'dp')]
    dot_general x72 -> x1, matrix products: 73.7 us -> 4.74 us  [on_device(): jnp.einsum('rd,jdc->jrc', normed, planes, preferred_element_type=F32)]
    pallas_call x0 -> x4, Pallas kernels: none -> 27.9 us  [the longest x1 16.7 us: mixer(): pl.pallas_call(mixer_kernel, grid=(heads,), out_shape=(jax.ShapeDtypeStru...]
    all_to_all x0 -> x2, starting transfers between devices: none -> 14.6 us  [the longest x1 7.74 us: on_device(): arrived = lax.all_to_all(packed, 'dp', 0, 0)]
    reduce_scatter x2 -> x0, waiting for transfers between devices: 14.3 us -> none  [reduce_features(): lax.psum_scatter(partial_rows, 'tensor', scatter_dimension=1, tiled=True)]
    mul x4 -> x0, other arithmetic: 13.9 us -> none  [the longest x1 9.18 us: mixer(): activated = jax.nn.silu(convolved)]
    reduce_sum x16 -> x0, other arithmetic: 10.5 us -> none  [the longest x12 6.85 us: mesa_block(): norm_next = jnp.sum(residual * residual, axis=-1, keepdims=True)]
    unnamed x26 -> x20, local copies, waits for them, and re-layouts: 12.3 us -> 4.64 us
  transfers between devices with their start and end apart: 5 -> 5, of which waited for: 5 -> 3; matrix products, arithmetic and copies ran while one was open for 10% -> 29% of each run, Pallas kernels for 0% -> 2%
where the time goes in v1:
time: 85 us; the launch traced here: 84.4 us
  Pallas kernels  27.9 us (33%)
  local copies, waits for them, and re-layouts  20.3 us (24%)
  starting transfers between devices  15.4 us (18%)
  waiting for transfers between devices  10.4 us (12%)
  matrix products  4.74 us (6%)
  other arithmetic  3.63 us (4%)
  between operations  2.05 us (2%)
    pallas_call x1, Pallas kernels, mixer(): pl.pallas_call(mixer_kernel, grid=(heads,), out_shape=(jax.ShapeDtypeStru...  16.7 us
    slice x1, local copies, waits for them, and re-layouts, on_device(): gate_up_weight[:, 1, :]  9.33 us
    all_to_all x1, starting transfers between devices, on_device(): arrived = lax.all_to_all(packed, 'dp', 0, 0)  7.74 us
    pallas_call x1, Pallas kernels, feed(): pl.pallas_call(feed_kernel, out_shape=(jax.ShapeDtypeStruct(mine.shape, B...  7.55 us
    all_to_all x1, starting transfers between devices, on_device(): prefix = lax.all_to_all(route(prefix_owner, arrived), 'dp', 0, 0)  6.9 us
    all_to_all x1, waiting for transfers between devices, on_device(): prefix = lax.all_to_all(route(prefix_owner, arrived), 'dp', 0, 0)  6.06 us
    squeeze x1, local copies, waits for them, and re-layouts, on_device(): gate_up_weight[:, 1, :]  5.13 us
    dot_general x1, matrix products, on_device(): jnp.einsum('rd,jdc->jrc', normed, planes, preferred_element_type=F32)  4.74 us
  transfers between devices with their start and end apart: 5, of which 3 were waited for; matrix products, arithmetic and copies ran while one was open for 29% of the time, Pallas kernels for 2%

profile of v1, /device:TPU:0, one launch (start us, length us, event | category | flops | bytes accessed | tf_op | source)
XLA Modules:
  0.0 84.4 jit_solution(13675136562279748696)
XLA Ops:
  0.6 0.6 collective-permute-start
  1.2 1.6 %copy.26 = f32[1,3,3,512]{3,2,0,1:T(4,128)} copy(f32[1,3,3,512]{3,0,2,1:T(1,128)} %param.24) | data formatting | bytes 36864
  3.5 1.8 %pack.1 = bf16[16,72,128]{2,1,0:T(8,128)(2,1)} custom-call(s32[1]{0:T(128)S(6)} %copy.28.group, f32[4,2,128,128]{3,2,1,0:T(8,128)} %bitcast.26, f32[3,3,512]{2,1,0:T(4,128)} %bitcast.27), custom_call_target="tpu_custom_call" | custom-call | tf_op jit(solution)/shard_map/pack/pallas_call | solution.py:68
  5.3 7.7 %all-to-all-start = ((bf16[16,72,128]{2,1,0:T(8,128)(2,1)}), bf16[16,72,128]{2,1,0:T(8,128)(2,1)S(1)}, u32[]{:S(2)}, u32[]{:S(2)}) async-start(bf16[16,72,128]{2,1,0:T(8,128)(2,1)} %pack.1), calls=%async_computation | async-start | bytes 589824 | tf_op jit(solution)/shard_map/all_to_all | solution.py:362
  13.0 9.3 %fusion.13 = (bf16[1024,1,768]{2,1,0:T(2,128)(2,1)}, bf16[1024,1,768]{2,1,0:T(2,128)(2,1)}) fusion(bf16[1024,2,768]{2,1,0:T(2,128)(2,1)} %param.21), kind=kLoop, calls=%fused_computation.21 | loop fusion | bytes 6291456 | tf_op jit(solution)/shard_map/slice | solution.py:364
  23.0 0.6 broadcast_in_dim_squeeze.3.decay
  23.6 5.1 %copy_bitcast_fusion = (bf16[1024,768]{1,0:T(8,128)(2,1)}, bf16[1024,768]{1,0:T(8,128)(2,1)}) fusion(bf16[1024,1,768]{2,1,0:T(2,128)(2,1)} %get-tuple-element.22, bf16[1024,1,768]{2,1,0:T(2,128)(2,1)} %get-tuple-element.23), kind=kLoop, calls=%fused_computation.8 | loop fusion | bytes 6291456 | tf_op jit(solution)/shard_map/squeeze | solution.py:364
  28.8 0.6 fusion.14
  29.4 1.2 %broadcast_select_fusion.1 = (bf16[512,512]{1,0:T(8,128)(2,1)S(1)}, bf16[512,512]{1,0:T(8,128)(2,1)S(1)}) fusion(bf16[512,512]{1,0:T(8,128)(2,1)S(1)} %copy-done.1, bf16[512,512]{1,0:T(8,128)(2,1)} %collective-permute-done.theirs, pred[]{:T(512)S(6)} %eq.3), kind=kLoop, calls=%fused_computation.16 | loop fusion | flops 524288 | bytes 2097153 | tf_op jit(solution)/shard_map/jit(_where)/select_n | solution.py:368
  30.6 0.8 copy-done.2
  31.3 0.2 copy-done.3
  31.5 0.3 fusion.2
  31.8 0.7 copy-done.5
  32.5 1.9 %route.1 = bf16[16,72,128]{2,1,0:T(8,128)(2,1)} custom-call(s32[4]{0:T(128)} %owners.1, bf16[16,72,128]{2,1,0:T(8,128)(2,1)} %copy-done.5), custom_call_target="tpu_custom_call" | custom-call | tf_op jit(solution)/shard_map/route/pallas_call | solution.py:98
  34.4 6.9 %all-to-all-start.1 = ((bf16[16,72,128]{2,1,0:T(8,128)(2,1)}), bf16[16,72,128]{2,1,0:T(8,128)(2,1)S(1)}, u32[]{:S(2)}, u32[]{:S(2)}) async-start(bf16[16,72,128]{2,1,0:T(8,128)(2,1)} %route.1), calls=%async_computation.1 | async-start | bytes 589824 | tf_op jit(solution)/shard_map/all_to_all | solution.py:366
  41.3 4.7 %fusion.5.query_in.key_in.value_in = f32[3,512,512]{2,1,0:T(8,128)} fusion(bf16[1024,3,512]{2,0,1:T(8,128)(2,1)S(1)} %copy-done, f32[1024]{0:T(1024)S(1)} %bitcast.30, f32[512]{0:T(512)S(1)} %add_rsqrt_fusion, bf16[512,512]{1,0:T(8,128)(2,1)} %copy-done.3, bf16[512,512]{1,0:T(8,128)(2,1)} %copy-done.2), kind=kOutput, calls=%fused_computation.7 | convolution fusion | flops 1614282752 | bytes 7346176 | tf_op jit(solution)/shard_map/rd,jdc->jrc/dot_general | solution.py:372
  46.0 6.1 %all-to-all-done.1.prefix = bf16[16,72,128]{2,1,0:T(8,128)(2,1)S(1)} async-done(((bf16[16,72,128]{2,1,0:T(8,128)(2,1)}), bf16[16,72,128]{2,1,0:T(8,128)(2,1)S(1)}, u32[]{:S(2)}, u32[]{:S(2)}) %all-to-all-start.1) | async-done | bytes 294944 | tf_op jit(solution)/shard_map/all_to_all | solution.py:366
  52.1 0.7 copy-done.4
  52.8 16.7 %mixer.1 = (bf16[512,1024]{1,0:T(8,128)(2,1)}, f32[4,2,128,128]{3,2,1,0:T(8,128)}, f32[3,3,512]{2,1,0:T(4,128)}) custom-call(s32[1]{0:T(128)} %copy.27.length_ref, f32[3,512,512]{2,1,0:T(8,128)} %fusion.5.query_in.key_in.value_in, f32[3,512,512]{2,1,0:T(8,128)} %fusion.5.query_in.key_in.value_in, f32[3,512,512]{2,1,0:T(8,128)} %fusion.5.query_in.key_in.value_in, ...), custom_call_target="tpu_custom_call" | custom-call | tf_op jit(solution)/shard_map/mixer/pallas_call | solution.py:251
  69.6 3.0 %collective-permute-done.1.arrived = bf16[512,1024]{1,0:T(8,128)(2,1)} collective-permute-done((bf16[512,1024]{1,0:T(8,128)(2,1)}, bf16[512,1024]{1,0:T(8,128)(2,1)}, u32[]{:S(2)}, u32[]{:S(2)}) %collective-permute-start.1) | collective-permute-done | bytes 1048608 | tf_op jit(solution)/shard_map/ppermute | solution.py:25
  72.5 7.5 %feed.1 = (bf16[512,512]{1,0:T(8,128)(2,1)}, f32[512,512]{1,0:T(8,128)}) custom-call(s32[1]{0:T(128)} %bitcast.1.core, bf16[512,512]{1,0:T(8,128)(2,1)} %mine.1, bf16[512,512]{1,0:T(8,128)(2,1)} %collective-permute-done.theirs, bf16[512,1024]{1,0:T(8,128)(2,1)} %get-tuple-element.12.partial, bf16[512,1024]{1,0:T(8,128)(2,1)} %collective-permute-done.1.arrived, ...), custom_call_target="tpu_custom_call" | custom-call | tf_op jit(solution)/shard_map/feed/pallas_call | solution.py:329
  80.2 0.6 copy.19
  80.9 1.4 %collective-permute-done.2 = bf16[512,512]{1,0:T(8,128)(2,1)S(1)} collective-permute-done((bf16[512,512]{1,0:T(8,128)(2,1)}, bf16[512,512]{1,0:T(8,128)(2,1)S(1)}, u32[]{:S(2)}, u32[]{:S(2)}) %collective-permute-start.2) | collective-permute-done | bytes 524320 | tf_op jit(solution)/shard_map/ppermute | solution.py:25
  82.2 2.2 %select_convert_fusion = bf16[512,512]{1,0:T(8,128)(2,1)} fusion(f32[512,512]{1,0:T(8,128)} %get-tuple-element.15, bf16[512,512]{1,0:T(8,128)(2,1)S(1)} %collective-permute-done.2, pred[512]{0:T(512)(128)(4,1)S(1)} %iota_compare_fusion), kind=kLoop, calls=%fused_computation.12 | loop fusion | flops 1048576 | bytes 2097664 | tf_op jit(solution)/shard_map/convert_element_type | solution.py:395
  (20 shorter events, 0.3 us)
Async XLA Ops:
  0.6 40.7 %copy-start = (bf16[1024,3,512]{2,0,1:T(8,128)(2,1)S(1)}, bf16[1024,3,512]{2,0,1:T(8,128)(2,1)}, u32[]{:S(2)}) copy-start(bf16[1024,3,512]{2,0,1:T(8,128)(2,1)} %param.16) | copy-start | bytes 9437188
  0.6 28.7 %collective-permute-start = (bf16[512,512]{1,0:T(8,128)(2,1)}, bf16[512,512]{1,0:T(8,128)(2,1)}, u32[]{:S(2)}, u32[]{:S(2)}) collective-permute-start(bf16[512,512]{1,0:T(8,128)(2,1)} %mine.1), channel_id=1, source_target_pairs={{0,1},{1,0},{2,3},{3,2},{4,5},{5,4},{6,7},{7,6},{8,9},{9,8},{10,11... | collective-permute-start | bytes 1572872 | tf_op jit(solution)/shard_map/ppermute | solution.py:25
  5.3 26.5 %all-to-all-start = ((bf16[16,72,128]{2,1,0:T(8,128)(2,1)}), bf16[16,72,128]{2,1,0:T(8,128)(2,1)S(1)}, u32[]{:S(2)}, u32[]{:S(2)}) async-start(bf16[16,72,128]{2,1,0:T(8,128)(2,1)} %pack.1), calls=%async_computation | async-start | bytes 589824 | tf_op jit(solution)/shard_map/all_to_all | solution.py:362
  13.0 10.0 %copy-start.7 = (f32[1,4,512]{2,1,0:T(4,128)S(1)}, f32[1,4,512]{2,1,0:T(4,128)}, u32[]{:S(2)}) copy-start(f32[1,4,512]{2,1,0:T(4,128)} %param.18) | copy-start | bytes 24580
  23.6 5.1 %copy-start.8 = (f32[2,1024]{1,0:T(2,128)S(1)}, f32[2,1024]{1,0:T(2,128)}, u32[]{:S(2)}) copy-start(f32[2,1024]{1,0:T(2,128)} %param.15) | copy-start | bytes 24580
  23.6 5.7 %copy-start.1 = (bf16[512,512]{1,0:T(8,128)(2,1)S(1)}, bf16[512,512]{1,0:T(8,128)(2,1)}, u32[]{:S(2)}) copy-start(bf16[512,512]{1,0:T(8,128)(2,1)} %mine.1) | copy-start | bytes 1572868
  30.5 0.8 copy-start.2
  30.6 1.0 %copy-start.3 = (bf16[512,512]{1,0:T(8,128)(2,1)}, bf16[512,512]{1,0:T(8,128)(2,1)S(1)}, u32[]{:S(2)}) copy-start(bf16[512,512]{1,0:T(8,128)(2,1)S(1)} %get-tuple-element.25) | copy-start | bytes 1572868
  31.8 0.7 copy-start.5
  34.4 17.7 %all-to-all-start.1 = ((bf16[16,72,128]{2,1,0:T(8,128)(2,1)}), bf16[16,72,128]{2,1,0:T(8,128)(2,1)S(1)}, u32[]{:S(2)}, u32[]{:S(2)}) async-start(bf16[16,72,128]{2,1,0:T(8,128)(2,1)} %route.1), calls=%async_computation.1 | async-start | bytes 589824 | tf_op jit(solution)/shard_map/all_to_all | solution.py:366
  52.1 0.7 copy-start.4
  69.5 3.1 %collective-permute-start.1 = (bf16[512,1024]{1,0:T(8,128)(2,1)}, bf16[512,1024]{1,0:T(8,128)(2,1)}, u32[]{:S(2)}, u32[]{:S(2)}) collective-permute-start(bf16[512,1024]{1,0:T(8,128)(2,1)} %get-tuple-element.12.partial), channel_id=1, source_target_pairs={{0,1},{1,0},{2,3},{3,2},{4,5},{5,4},{6,7},{7,6},{8,9},{9,8},{10,11... | collective-permute-start | bytes 3145736 | tf_op jit(solution)/shard_map/ppermute | solution.py:25
  72.5 7.7 %copy-start.6 = (f32[3,3,512]{2,1,0:T(4,128)S(1)}, f32[3,3,512]{2,1,0:T(4,128)}, u32[]{:S(2)}) copy-start(f32[3,3,512]{2,1,0:T(4,128)} %get-tuple-element.18) | copy-start | bytes 55300
  80.1 2.1 %collective-permute-start.2 = (bf16[512,512]{1,0:T(8,128)(2,1)}, bf16[512,512]{1,0:T(8,128)(2,1)S(1)}, u32[]{:S(2)}, u32[]{:S(2)}) collective-permute-start(bf16[512,512]{1,0:T(8,128)(2,1)} %get-tuple-element.16), channel_id=1, source_target_pairs={{0,1},{1,0},{2,3},{3,2},{4,5},{5,4},{6,7},{7,6},{8,9},{9,8},{10,11... | collective-permute-start | bytes 1572872 | tf_op jit(solution)/shard_map/ppermute | solution.py:25

commit v2 on v1

--- a/solution.py
+++ b/solution.py
@@ -56,7 +56,7 @@
             parts = [cache[head, plane, offset : offset + state_rows, :]]
             for index in range(piece * tail_rows, (piece + 1) * tail_rows):
                 if index < (CONV - 1) * 3:
-                    parts.append(tail[index // 3, index % 3 : index % 3 + 1, lanes])
+                    parts.append(tail[index // 3, index % 3, :, lanes])
                 else:
                     parts.append(tag)
             parts.append(jnp.broadcast_to(tag, (8 - tail_rows, LANES)))
@@ -147,7 +147,8 @@
             convolved = (
                 convolved + taps[part, tap : tap + 1, :] * extended[pl.ds(5 + tap, rows_total), :]
             )
-        tail_out[:, part, :] = extended[pl.ds(length + 5, CONV - 1), :]
+        for place in range(CONV - 1):
+            tail_out[place, part] = extended[pl.ds(length + 5 + place, 1), :]
         activated.append(convolved / (1.0 + jnp.exp(-convolved)))
     queries, key_rows, value_rows = activated
     queries = queries * lax.rsqrt(jnp.sum(queries * queries, axis=-1, keepdims=True) + 1e-06)
@@ -254,7 +255,7 @@
         out_shape=(
             jax.ShapeDtypeStruct((rows_total, features), BF16),
             jax.ShapeDtypeStruct((heads, 2, DK, DK), F32),
-            jax.ShapeDtypeStruct((CONV - 1, 3, width), F32),
+            jax.ShapeDtypeStruct((CONV - 1, 3, 1, width), F32),
         ),
         in_specs=[
             pl.BlockSpec(memory_space=pltpu.SMEM),
@@ -270,7 +271,7 @@
         out_specs=(
             pl.BlockSpec((rows_total, features), lambda head: (0, 0)),
             pl.BlockSpec((1, 2, DK, DK), lambda head: (head, 0, 0, 0)),
-            pl.BlockSpec((CONV - 1, 3, DK), lambda head: (0, 0, head)),
+            pl.BlockSpec((CONV - 1, 3, 1, DK), lambda head: (0, 0, 0, head)),
         ),
         scratch_shapes=[
             pltpu.VMEM((rows_total + 8, DK), F32),
@@ -291,53 +292,6 @@
     )
 
 
-def feed_kernel(core, mine, theirs, partial, arrived, gain, gate, up, down, leaving, kept):
-    half = mine.shape[1]
-    features = 2 * half
-    own = pl.multiple_of(core[0] * half, half)
-    far = pl.multiple_of((1 - core[0]) * half, half)
-
-    def middle(source, columns, rows):
-        added = partial[rows, columns].astype(F32) + arrived[rows, columns].astype(F32)
-        return (source[rows, :].astype(F32) + added).astype(BF16).astype(F32)
-
-    step = 256
-    for start in range(0, mine.shape[0], step):
-        rows = slice(start, start + step)
-        middle_own = middle(mine, pl.ds(own, half), rows)
-        middle_far = middle(theirs, pl.ds(far, half), rows)
-        squares = jnp.sum(
-            middle_own * middle_own + middle_far * middle_far, axis=-1, keepdims=True
-        )
-        inverse = lax.rsqrt(squares * (1.0 / features) + 1e-05)
-        normed_own = (middle_own * inverse * gain[:, pl.ds(own, half)]).astype(BF16)
-        normed_far = (middle_far * inverse * gain[:, pl.ds(far, half)]).astype(BF16)
-
-        def through(weight):
-            return dot_nn(normed_own, weight[pl.ds(own, half), :]) + dot_nn(
-                normed_far, weight[pl.ds(far, half), :]
-            )
-
-        gated = through(gate)
-        hidden = (gated / (1.0 + jnp.exp(-gated)) * through(up)).astype(BF16)
-        leaving[rows, :] = dot_nn(hidden, down[:, pl.ds(far, half)]).astype(BF16)
-        kept[rows, :] = dot_nn(hidden, down[:, pl.ds(own, half)]) + middle_own
-
-
-def feed(core, mine, theirs, partial, arrived, gain, gate, up, down):
-    vmem = pl.BlockSpec(memory_space=pltpu.VMEM)
-    return pl.pallas_call(
-        feed_kernel,
-        out_shape=(
-            jax.ShapeDtypeStruct(mine.shape, BF16),
-            jax.ShapeDtypeStruct(mine.shape, F32),
-        ),
-        in_specs=[pl.BlockSpec(memory_space=pltpu.SMEM)] + [vmem] * 8,
-        out_specs=(vmem, vmem),
-        name="feed",
-    )(core, mine, theirs, partial, arrived, gain, gate, up, down)
-
-
 def on_device(
     tokens,
     norm_gains,
@@ -354,22 +308,29 @@
     request_group,
     prefix_owner,
 ):
-    rows_total = tokens.shape[0]
-    core = lax.axis_index("tensor")
-    first = core == 0
-    packed = pack(prefix_cache[0], prefix_tail[0], request_group, lax.axis_size("dp"))
+    rows_total, half = tokens.shape
+    first = lax.axis_index("tensor") == 0
+    packed = pack(
+        prefix_cache[0],
+        jnp.transpose(prefix_tail, (1, 2, 0, 3)),
+        request_group,
+        lax.axis_size("dp"),
+    )
     theirs = other_core(tokens)
     arrived = lax.all_to_all(packed, "dp", 0, 0)
-    arrived, gate_weight, up_weight = lax.optimization_barrier(
-        (arrived, gate_up_weight[:, 0, :], gate_up_weight[:, 1, :])
-    )
-    prefix = lax.all_to_all(route(prefix_owner, arrived), "dp", 0, 0)
     whole_rows = jnp.concatenate(
         [jnp.where(first, tokens, theirs), jnp.where(first, theirs, tokens)], axis=1
     ).astype(F32)
     normed = rms_rows(whole_rows, norm_gains[0])
     planes = jnp.transpose(qkv_weight, (1, 0, 2))
     projected = jnp.einsum("rd,jdc->jrc", normed, planes, preferred_element_type=F32)
+    arrived, projected, gate_up_weight = lax.optimization_barrier(
+        (arrived, projected, gate_up_weight)
+    )
+    prefix = lax.all_to_all(route(prefix_owner, arrived), "dp", 0, 0)
+    prefix, gate_up_matrix = lax.optimization_barrier(
+        (prefix, gate_up_weight.reshape(gate_up_weight.shape[0], -1))
+    )
     partial, state_out, tail_out = mixer(
         projected,
         jnp.transpose(conv_weight, (1, 0, 2)),
@@ -379,21 +340,21 @@
         out_weight,
         suffix_len,
     )
-    leaving, kept = feed(
-        core.reshape(1).astype(jnp.int32),
-        tokens,
-        theirs,
-        partial,
-        other_core(partial),
-        norm_gains[1:2],
-        gate_weight,
-        up_weight,
-        down_weight,
-    )
+    attended = partial.astype(F32) + other_core(partial).astype(F32)
+    middle = (whole_rows + attended).astype(BF16)
+    gate_up = jnp.dot(
+        rms_rows(middle.astype(F32), norm_gains[1]), gate_up_matrix, preferred_element_type=F32
+    )
+    hidden_width = gate_up.shape[1] // 2
+    hidden = (jax.nn.silu(gate_up[:, :hidden_width]) * gate_up[:, hidden_width:]).astype(BF16)
+    forward = jnp.dot(hidden, down_weight, preferred_element_type=F32)
+    left, right = forward[:, :half], forward[:, half:]
+    leaving = other_core(jnp.where(first, right, left).astype(BF16))
+    kept = jnp.where(first, left, right) + leaving.astype(F32)
+    base = jnp.where(first, middle[:, :half], middle[:, half:]).astype(F32)
     live_rows = jnp.arange(rows_total) < suffix_len[0]
-    result = kept + other_core(leaving).astype(F32)
-    result = jnp.where(live_rows[:, None], result, 0.0).astype(BF16)
-    return (result, state_out[None], tail_out[None])
+    result = jnp.where(live_rows[:, None], base + kept, 0.0).astype(BF16)
+    return (result, state_out[None], jnp.transpose(tail_out, (2, 0, 1, 3)))
 
 
 def solution(mesh):

time: 85 us -> 68.5 us (0.81)
  local copies, waits for them, and re-layouts: 20.3 us -> 7.61 us
  Pallas kernels: 27.9 us -> 20.3 us
  waiting for transfers between devices: 10.4 us -> 14.1 us
  starting transfers between devices: 15.4 us -> 12.2 us
  matrix products: 4.74 us -> 6.48 us
  other arithmetic: 3.63 us -> 4.91 us
    slice x2 -> x1, local copies, waits for them, and re-layouts: 9.93 us -> 0.78 us  [on_device(): norm_gains[1]]
    pallas_call x1 -> x0, Pallas kernels: 7.55 us -> none  [feed(): pl.pallas_call(feed_kernel, out_shape=(jax.ShapeDtypeStruct(mine.shape, B...]
    squeeze x1 -> x0, local copies, waits for them, and re-layouts: 5.13 us -> none  [on_device(): gate_up_weight[:, 1, :]]
    all_to_all x1, waiting for transfers between devices: 0.01 us -> 4.7 us  [on_device(): arrived = lax.all_to_all(packed, 'dp', 0, 0)]
    all_to_all x1, starting transfers between devices: 6.9 us -> 3.54 us  [on_device(): prefix = lax.all_to_all(route(prefix_owner, arrived), 'dp', 0, 0)]
    dot_general x0 -> x2, matrix products: none -> 2.92 us  [the longest x1 1.9 us: on_device(): jnp.dot(rms_rows(middle.astype(F32), norm_gains[1]), gate_up_matrix, pref...]
    reduce_sum x1 -> x2, other arithmetic: 0.28 us -> 2.42 us  [rms_rows(): jnp.mean(floats * floats, axis=-1, keepdims=True) + 1e-05]
    unnamed x20 -> x17, local copies, waits for them, and re-layouts: 4.64 us -> 6.23 us
  transfers between devices with their start and end apart: 5 -> 5, of which waited for: 3 -> 4; matrix products, arithmetic and copies ran while one was open for 29% -> 16% of each run, Pallas kernels for 2% -> 3%
where the time goes in v2:
time: 68.5 us; the launch traced here: 68 us
  Pallas kernels  20.3 us (30%)
  waiting for transfers between devices  14.1 us (21%)
  starting transfers between devices  12.2 us (18%)
  local copies, waits for them, and re-layouts  7.61 us (11%)
  matrix products  6.48 us (9%)
  other arithmetic  4.91 us (7%)
  between operations  2.35 us (3%)
    pallas_call x1, Pallas kernels, mixer(): pl.pallas_call(mixer_kernel, grid=(heads,), out_shape=(jax.ShapeDtypeStru...  16.7 us
    all_to_all x1, starting transfers between devices, on_device(): arrived = lax.all_to_all(packed, 'dp', 0, 0)  7.81 us
    unnamed x17, local copies, waits for them, and re-layouts  6.23 us
    all_to_all x1, waiting for transfers between devices, on_device(): prefix = lax.all_to_all(route(prefix_owner, arrived), 'dp', 0, 0)  4.79 us
    all_to_all x1, waiting for transfers between devices, on_device(): arrived = lax.all_to_all(packed, 'dp', 0, 0)  4.7 us
    ppermute x3, waiting for transfers between devices, other_core(): return lax.ppermute(array_in, 'tensor', [(0, 1), (1, 0)])  4.63 us
    dot_general x1, matrix products, on_device(): jnp.einsum('rd,jdc->jrc', normed, planes, preferred_element_type=F32)  3.57 us
    all_to_all x1, starting transfers between devices, on_device(): prefix = lax.all_to_all(route(prefix_owner, arrived), 'dp', 0, 0)  3.54 us
  transfers between devices with their start and end apart: 5, of which 4 were waited for; matrix products, arithmetic and copies ran while one was open for 16% of the time, Pallas kernels for 3%

profile of v2, /device:TPU:0, one launch (start us, length us, event | category | flops | bytes accessed | tf_op | source)
XLA Modules:
  0.0 68.0 jit_solution(8728249947680544861)
XLA Ops:
  0.6 0.6 collective-permute-start
  2.1 1.8 %pack.1 = bf16[16,72,128]{2,1,0:T(8,128)(2,1)} custom-call(s32[1]{0:T(128)S(6)} %copy.19.group, f32[4,2,128,128]{3,2,1,0:T(8,128)} %bitcast.26, f32[3,3,1,512]{3,2,1,0:T(1,128)} %bitcast.28), custom_call_target="tpu_custom_call" | custom-call | tf_op jit(solution)/shard_map/pack/pallas_call | solution.py:68
  3.9 7.8 %all-to-all-start = ((bf16[16,72,128]{2,1,0:T(8,128)(2,1)}), bf16[16,72,128]{2,1,0:T(8,128)(2,1)S(1)}, u32[]{:S(2)}, u32[]{:S(2)}) async-start(bf16[16,72,128]{2,1,0:T(8,128)(2,1)} %pack.1), calls=%async_computation | async-start | bytes 589824 | tf_op jit(solution)/shard_map/all_to_all | solution.py:320
  11.7 0.8 %fusion.26 = (f32[1,1024]{1,0:T(1,128)S(1)}, f32[1,1024]{1,0:T(1,128)S(1)}) fusion(f32[2,1024]{1,0:T(2,128)} %param.15), kind=kLoop, calls=%fused_computation.35 | loop fusion | bytes 16384 | tf_op jit(solution)/shard_map/slice | solution.py:346
  12.5 1.3 %broadcast_select_fusion.1 = (bf16[512,512]{1,0:T(8,128)(2,1)S(1)}, bf16[512,512]{1,0:T(8,128)(2,1)S(1)}) fusion(bf16[512,512]{1,0:T(8,128)(2,1)} %param.14, bf16[512,512]{1,0:T(8,128)(2,1)} %collective-permute-done, pred[]{:T(512)S(6)} %eq.3), kind=kLoop, calls=%fused_computation.29 | loop fusion | flops 524288 | bytes 2097153 | tf_op jit(solution)/shard_map/jit(_where)/select_n | solution.py:322
  13.8 0.3 fusion.5
  14.1 0.5 copy-done.1
  14.8 3.6 %fusion.9.query_in.key_in.value_in = f32[3,512,512]{2,1,0:T(8,128)} fusion(bf16[1024,3,512]{2,0,1:T(8,128)(2,1)S(1)} %copy-done, f32[1024]{0:T(1024)S(1)} %bitcast.30, f32[512]{0:T(512)S(1)} %add_rsqrt_fusion.1, bf16[512,512]{1,0:T(8,128)(2,1)S(1)} %get-tuple-element.22, bf16[512,512]{1,0:T(8,128)(2,1)S(1)} %get-tuple-element.21), kind=kOutput, calls=%fused_computation.14 | convolution fusion | flops 1614282752 | bytes 7346176 | tf_op jit(solution)/shard_map/rd,jdc->jrc/dot_general | solution.py:326
  18.4 4.7 %all-to-all-done.arrived = bf16[16,72,128]{2,1,0:T(8,128)(2,1)S(1)} async-done(((bf16[16,72,128]{2,1,0:T(8,128)(2,1)}), bf16[16,72,128]{2,1,0:T(8,128)(2,1)S(1)}, u32[]{:S(2)}, u32[]{:S(2)}) %all-to-all-start) | async-done | bytes 294944 | tf_op jit(solution)/shard_map/all_to_all | solution.py:320
  23.1 0.7 %copy-done.5 = bf16[16,72,128]{2,1,0:T(8,128)(2,1)} copy-done((bf16[16,72,128]{2,1,0:T(8,128)(2,1)}, bf16[16,72,128]{2,1,0:T(8,128)(2,1)S(1)}, u32[]{:S(2)}) %copy-start.5) | copy-done | bytes 294936
  23.8 1.9 %route.1 = bf16[16,72,128]{2,1,0:T(8,128)(2,1)} custom-call(s32[4]{0:T(128)} %owners.1, bf16[16,72,128]{2,1,0:T(8,128)(2,1)} %copy-done.5), custom_call_target="tpu_custom_call" | custom-call | tf_op jit(solution)/shard_map/route/pallas_call | solution.py:98
  25.7 3.5 %all-to-all-start.1 = ((bf16[16,72,128]{2,1,0:T(8,128)(2,1)}), bf16[16,72,128]{2,1,0:T(8,128)(2,1)S(1)}, u32[]{:S(2)}, u32[]{:S(2)}) async-start(bf16[16,72,128]{2,1,0:T(8,128)(2,1)} %route.1), calls=%async_computation.1 | async-start | bytes 589824 | tf_op jit(solution)/shard_map/all_to_all | solution.py:330
  29.9 0.6 broadcast_in_dim_squeeze.3.decay
  30.5 4.1 %copy.17 = bf16[128,8,2,768]{3,1,2,0:T(8,128)(2,1)} copy(bf16[128,8,2,768]{3,2,1,0:T(2,128)(2,1)} %bitcast.24) | data formatting | bytes 6291456
  34.6 4.8 %all-to-all-done.1.prefix = bf16[16,72,128]{2,1,0:T(8,128)(2,1)S(1)} async-done(((bf16[16,72,128]{2,1,0:T(8,128)(2,1)}), bf16[16,72,128]{2,1,0:T(8,128)(2,1)S(1)}, u32[]{:S(2)}, u32[]{:S(2)}) %all-to-all-start.1) | async-done | bytes 294944 | tf_op jit(solution)/shard_map/all_to_all | solution.py:330
  39.4 0.7 %copy-done.4 = bf16[16,72,128]{2,1,0:T(8,128)(2,1)} copy-done((bf16[16,72,128]{2,1,0:T(8,128)(2,1)}, bf16[16,72,128]{2,1,0:T(8,128)(2,1)S(1)}, u32[]{:S(2)}) %copy-start.4) | copy-done | bytes 294936
  40.1 16.7 %mixer.1 = (bf16[512,1024]{1,0:T(8,128)(2,1)}, f32[4,2,128,128]{3,2,1,0:T(8,128)}, f32[3,3,1,512]{3,2,1,0:T(1,128)}) custom-call(s32[1]{0:T(128)} %copy.18.length_ref, f32[3,512,512]{2,1,0:T(8,128)} %fusion.9.query_in.key_in.value_in, f32[3,512,512]{2,1,0:T(8,128)} %fusion.9.query_in.key_in.value_in, f32[3,512,512]{2,1,0:T(8,128)} %fusion.9.query_in.key_in.value_in, ...), custom_call_target="tpu_custom_call" | custom-call | tf_op jit(solution)/shard_map/mixer/pallas_call | solution.py:252
  56.8 2.9 %collective-permute-done.1 = bf16[512,1024]{1,0:T(8,128)(2,1)S(1)} collective-permute-done((bf16[512,1024]{1,0:T(8,128)(2,1)}, bf16[512,1024]{1,0:T(8,128)(2,1)S(1)}, u32[]{:S(2)}, u32[]{:S(2)}) %collective-permute-start.1) | collective-permute-done | bytes 1048608 | tf_op jit(solution)/shard_map/ppermute | solution.py:25
  59.7 2.1 %fusion.2 = (f32[512]{0:T(512)S(1)}, bf16[512,1024]{1,0:T(8,128)(2,1)S(1)}) fusion(bf16[512,1024]{1,0:T(8,128)(2,1)S(1)} %collective-permute-done.1, bf16[512,1024]{1,0:T(8,128)(2,1)} %get-tuple-element.15, bf16[512,512]{1,0:T(8,128)(2,1)} %copy-done.2, bf16[512,512]{1,0:T(8,128)(2,1)} %copy-done.1), kind=kLoop, calls=%fused_computation.7 | loop fusion | flops 6290944 | bytes 4196352 | tf_op jit(solution)/shard_map/reduce_sum | solution.py:20
  61.9 1.9 %fusion.15 = f32[512,1536]{1,0:T(8,128)S(1)} fusion(bf16[1024,1536]{1,0:T(8,128)(2,1)S(1)} %bitcast.25, bf16[512,1024]{1,0:T(8,128)(2,1)S(1)} %get-tuple-element.20, f32[1024]{0:T(1024)S(1)} %bitcast.29, f32[512]{0:T(512)S(1)} %add_rsqrt_fusion), kind=kOutput, calls=%fused_computation.18 | convolution fusion | flops 1612709888 | bytes 7346176 | tf_op jit(solution)/shard_map/dot_general | solution.py:345
  63.8 1.0 %fusion.21 = f32[512,1024]{1,0:T(8,128)S(1)} fusion(bf16[768,1024]{1,0:T(8,128)(2,1)S(1)} %copy-done.7, f32[512,1536]{1,0:T(8,128)S(1)} %fusion.15), kind=kOutput, calls=%fused_computation.26 | convolution fusion | flops 807665664 | bytes 6815744 | tf_op jit(solution)/shard_map/dot_general | solution.py:350
  64.9 0.2 collective-permute-start.2
  65.1 1.8 %collective-permute-done.2 = bf16[512,512]{1,0:T(8,128)(2,1)S(1)} collective-permute-done((bf16[512,512]{1,0:T(8,128)(2,1)S(1)}, bf16[512,512]{1,0:T(8,128)(2,1)S(1)}, u32[]{:S(2)}, u32[]{:S(2)}) %collective-permute-start.2) | collective-permute-done | bytes 524320 | tf_op jit(solution)/shard_map/ppermute | solution.py:25
  66.9 1.1 %select_convert_fusion = bf16[512,512]{1,0:T(8,128)(2,1)} fusion(bf16[512,512]{1,0:T(8,128)(2,1)S(1)} %collective-permute-done.2, f32[512,1024]{1,0:T(8,128)S(1)} %fusion.21, bf16[512,1024]{1,0:T(8,128)(2,1)S(1)} %get-tuple-element.20, pred[512]{0:T(512)(128)(4,1)S(1)} %iota_compare_fusion, pred[]{:T(512)S(6)} %eq.3), kind=kLoop, calls=%fused_computation.20 | loop fusion | flops 2097152 | bytes 4194817 | tf_op jit(solution)/shard_map/convert_element_type | solution.py:356
  (19 shorter events, 0.4 us)
Async XLA Ops:
  0.6 14.2 %copy-start = (bf16[1024,3,512]{2,0,1:T(8,128)(2,1)S(1)}, bf16[1024,3,512]{2,0,1:T(8,128)(2,1)}, u32[]{:S(2)}) copy-start(bf16[1024,3,512]{2,0,1:T(8,128)(2,1)} %param.16) | copy-start | bytes 9437188
  0.6 11.9 %collective-permute-start = (bf16[512,512]{1,0:T(8,128)(2,1)}, bf16[512,512]{1,0:T(8,128)(2,1)}, u32[]{:S(2)}, u32[]{:S(2)}) collective-permute-start(bf16[512,512]{1,0:T(8,128)(2,1)} %param.14), channel_id=1, source_target_pairs={{0,1},{1,0},{2,3},{3,2},{4,5},{5,4},{6,7},{7,6},{8,9},{9,8},{10,11... | collective-permute-start | bytes 1572872 | tf_op jit(solution)/shard_map/ppermute | solution.py:25
  3.9 19.1 %all-to-all-start = ((bf16[16,72,128]{2,1,0:T(8,128)(2,1)}), bf16[16,72,128]{2,1,0:T(8,128)(2,1)S(1)}, u32[]{:S(2)}, u32[]{:S(2)}) async-start(bf16[16,72,128]{2,1,0:T(8,128)(2,1)} %pack.1), calls=%async_computation | async-start | bytes 589824 | tf_op jit(solution)/shard_map/all_to_all | solution.py:320
  13.8 0.8 %copy-start.1 = (bf16[512,512]{1,0:T(8,128)(2,1)}, bf16[512,512]{1,0:T(8,128)(2,1)S(1)}, u32[]{:S(2)}) copy-start(bf16[512,512]{1,0:T(8,128)(2,1)S(1)} %get-tuple-element.21) | copy-start | bytes 1572868
  13.8 1.0 %copy-start.2 = (bf16[512,512]{1,0:T(8,128)(2,1)}, bf16[512,512]{1,0:T(8,128)(2,1)S(1)}, u32[]{:S(2)}) copy-start(bf16[512,512]{1,0:T(8,128)(2,1)S(1)} %get-tuple-element.22) | copy-start | bytes 1572868
  14.8 15.1 %copy-start.6 = (f32[1,4,512]{2,1,0:T(4,128)S(1)}, f32[1,4,512]{2,1,0:T(4,128)}, u32[]{:S(2)}) copy-start(f32[1,4,512]{2,1,0:T(4,128)} %param.18) | copy-start | bytes 24580
  23.1 0.7 %copy-start.5 = (bf16[16,72,128]{2,1,0:T(8,128)(2,1)}, bf16[16,72,128]{2,1,0:T(8,128)(2,1)S(1)}, u32[]{:S(2)}) copy-start(bf16[16,72,128]{2,1,0:T(8,128)(2,1)S(1)} %all-to-all-done.arrived) | copy-start | bytes 884740
  25.7 13.7 %all-to-all-start.1 = ((bf16[16,72,128]{2,1,0:T(8,128)(2,1)}), bf16[16,72,128]{2,1,0:T(8,128)(2,1)S(1)}, u32[]{:S(2)}, u32[]{:S(2)}) async-start(bf16[16,72,128]{2,1,0:T(8,128)(2,1)} %route.1), calls=%async_computation.1 | async-start | bytes 589824 | tf_op jit(solution)/shard_map/all_to_all | solution.py:330
  39.4 0.7 %copy-start.4 = (bf16[16,72,128]{2,1,0:T(8,128)(2,1)}, bf16[16,72,128]{2,1,0:T(8,128)(2,1)S(1)}, u32[]{:S(2)}) copy-start(bf16[16,72,128]{2,1,0:T(8,128)(2,1)S(1)} %all-to-all-done.1.prefix) | copy-start | bytes 884740
  56.7 5.1 %copy-start.3 = (bf16[128,8,2,768]{3,1,2,0:T(8,128)(2,1)S(1)}, bf16[128,8,2,768]{3,1,2,0:T(8,128)(2,1)}, u32[]{:S(2)}) copy-start(bf16[128,8,2,768]{3,1,2,0:T(8,128)(2,1)} %copy.17) | copy-start | bytes 9437188
  56.8 2.9 %collective-permute-start.1 = (bf16[512,1024]{1,0:T(8,128)(2,1)}, bf16[512,1024]{1,0:T(8,128)(2,1)S(1)}, u32[]{:S(2)}, u32[]{:S(2)}) collective-permute-start(bf16[512,1024]{1,0:T(8,128)(2,1)} %get-tuple-element.15), channel_id=1, source_target_pairs={{0,1},{1,0},{2,3},{3,2},{4,5},{5,4},{6,7},{7,6},{8,9},{9,8},{10,11... | collective-permute-start | bytes 3145736 | tf_op jit(solution)/shard_map/ppermute | solution.py:25
  61.9 1.9 %copy-start.7 = (bf16[768,1024]{1,0:T(8,128)(2,1)S(1)}, bf16[768,1024]{1,0:T(8,128)(2,1)}, u32[]{:S(2)}) copy-start(bf16[768,1024]{1,0:T(8,128)(2,1)} %param.22) | copy-start | bytes 4718596
  64.9 2.0 %collective-permute-start.2 = (bf16[512,512]{1,0:T(8,128)(2,1)S(1)}, bf16[512,512]{1,0:T(8,128)(2,1)S(1)}, u32[]{:S(2)}, u32[]{:S(2)}) collective-permute-start(bf16[512,512]{1,0:T(8,128)(2,1)S(1)} %select_convert_fusion.1), channel_id=1, source_target_pairs={{0,1},{1,0},{2,3},{3,2},{4,5},{5,4},{6,7},{7,6},{8,9},{9,8},{10,11... | collective-permute-start | bytes 1572872 | tf_op jit(solution)/shard_map/ppermute | solution.py:25

commit v3 on v2

--- a/solution.py
+++ b/solution.py
@@ -125,116 +125,144 @@
 ):
     rows_total = query_in.shape[1]
     blocks = rows_total // BLOCK
-    head = pl.program_id(0)
+    step_id = pl.program_id(0)
     length = length_ref[0]
-    share, chunk_rows, _ = prefix.shape
-    state_rows = chunk_rows - 8
+    local_heads = regular.shape[0]
+    share = prefix.shape[0] // local_heads
+    state_rows = prefix.shape[1] - 8
     tail_rows = -(-(CONV - 1) * 3 // share)
-    chunks = [prefix[piece].astype(F32) for piece in range(share)]
-    state = jnp.concatenate([chunk[:state_rows] for chunk in chunks], axis=0)
-    hstate, gstate = state[:DK], state[DK:]
-
     live = lax.broadcasted_iota(jnp.int32, (rows_total, 1), 0) < length
-    activated = []
-    for part, source in enumerate((query_in, key_in, value_in)):
-        for before in range(CONV - 1):
-            piece, inside = divmod(before * 3 + part, tail_rows)
-            place = state_rows + inside
-            extended[5 + before : 6 + before, :] = chunks[piece][place : place + 1]
-        extended[8 : 8 + rows_total, :] = source[0]
-        convolved = taps[part, 0:1, :] * extended[pl.ds(5, rows_total), :]
-        for tap in range(1, CONV):
-            convolved = (
-                convolved + taps[part, tap : tap + 1, :] * extended[pl.ds(5 + tap, rows_total), :]
-            )
-        for place in range(CONV - 1):
-            tail_out[place, part] = extended[pl.ds(length + 5 + place, 1), :]
-        activated.append(convolved / (1.0 + jnp.exp(-convolved)))
-    queries, key_rows, value_rows = activated
-    queries = queries * lax.rsqrt(jnp.sum(queries * queries, axis=-1, keepdims=True) + 1e-06)
-    key_rows = key_rows * lax.rsqrt(jnp.sum(key_rows * key_rows, axis=-1, keepdims=True) + 1e-06)
-    key_rows = jnp.where(live, key_rows, 0.0)
-    value_rows = jnp.where(live, value_rows, 0.0)
-
     lane = lax.broadcasted_iota(jnp.int32, (BLOCK, BLOCK), 1)
     row = lax.broadcasted_iota(jnp.int32, (BLOCK, BLOCK), 0)
     causal = row >= lane
-    regular_row = regular[0]
-
-    operands = []
-    for block in range(blocks):
-        rows = slice(block * BLOCK, (block + 1) * BLOCK)
-        keys, values = key_rows[rows], value_rows[rows]
-        gates = decay[0, :, block * BLOCK : (block + 1) * BLOCK]
-        position = lax.broadcasted_iota(jnp.int32, (1, BLOCK), 1) + block * BLOCK
-        gates = jnp.where(position < length, gates, 0.0)
-        down = jnp.sum(jnp.where(causal, gates, 0.0), axis=1, keepdims=True)
-        wide = jnp.broadcast_to(down, (BLOCK, BLOCK))
-        differ = wide - wide.T
-        weights = jnp.where(causal, jnp.exp(jnp.minimum(differ, 0.0)), 0.0)
-        growth = jnp.exp(down)
-        last = down[BLOCK - 1 : BLOCK, :]
-        root_tail = jnp.exp(0.5 * (last - down))
-        decay_last = jnp.exp(last)
-        keys_high = keys.astype(BF16)
-        operands.append(
-            (
-                keys_high,
-                jnp.concatenate([hstate.astype(BF16), keys_high], axis=0),
-                gstate.astype(BF16),
-                values.astype(BF16),
-                weights,
-                growth,
+
+    chains = []
+    for local in range(local_heads):
+        lanes = slice(local * DK, (local + 1) * DK)
+        chunks = [prefix[local * share + piece].astype(F32) for piece in range(share)]
+        state = jnp.concatenate([chunk[:state_rows] for chunk in chunks], axis=0)
+        hstate, gstate = state[:DK], state[DK:]
+        activated = []
+        for part, source in enumerate((query_in, key_in, value_in)):
+            longer = extended.at[local * 3 + part]
+            for before in range(CONV - 1):
+                piece, inside = divmod(before * 3 + part, tail_rows)
+                place = state_rows + inside
+                longer[5 + before : 6 + before, :] = chunks[piece][place : place + 1]
+            longer[8 : 8 + rows_total, :] = source[0, :, lanes]
+            convolved = taps[part, 0:1, lanes] * longer[pl.ds(5, rows_total), :]
+            for tap in range(1, CONV):
+                convolved = (
+                    convolved
+                    + taps[part, tap : tap + 1, lanes] * longer[pl.ds(5 + tap, rows_total), :]
+                )
+            for place in range(CONV - 1):
+                tail_out[place, part, :, lanes] = longer[pl.ds(length + 5 + place, 1), :]
+            activated.append(convolved / (1.0 + jnp.exp(-convolved)))
+        queries, key_rows, value_rows = activated
+        queries = queries * lax.rsqrt(jnp.sum(queries * queries, axis=-1, keepdims=True) + 1e-06)
+        key_rows = key_rows * lax.rsqrt(
+            jnp.sum(key_rows * key_rows, axis=-1, keepdims=True) + 1e-06
+        )
+        key_rows = jnp.where(live, key_rows, 0.0)
+        value_rows = jnp.where(live, value_rows, 0.0)
+        for block in range(blocks):
+            rows = slice(block * BLOCK, (block + 1) * BLOCK)
+            keys, values = key_rows[rows], value_rows[rows]
+            gates = decay[local, :, block * BLOCK : (block + 1) * BLOCK]
+            position = lax.broadcasted_iota(jnp.int32, (1, BLOCK), 1) + block * BLOCK
+            gates = jnp.where(position < length, gates, 0.0)
+            down = jnp.sum(jnp.where(causal, gates, 0.0), axis=1, keepdims=True)
+            wide = jnp.broadcast_to(down, (BLOCK, BLOCK))
+            differ = wide - wide.T
+            weights = jnp.where(causal, jnp.exp(jnp.minimum(differ, 0.0)), 0.0)
+            growth = jnp.exp(wide)
+            last = down[BLOCK - 1 : BLOCK, :]
+            root_tail = jnp.exp(0.5 * (last - down))
+            decay_last = jnp.exp(last)
+            chains.append(
+                (
+                    queries[rows],
+                    keys.astype(BF16),
+                    jnp.concatenate([keys.T, hstate], axis=1).astype(BF16),
+                    gstate.astype(BF16),
+                    values.astype(BF16),
+                    weights,
+                    growth,
+                    regular[local],
+                )
             )
-        )
-        grown = jnp.concatenate([keys * root_tail, values * root_tail], axis=1).astype(BF16)
-        update = dot_tn(grown, grown[:, :DK])
-        hstate = decay_last * hstate + update[:DK]
-        gstate = decay_last * gstate + update[DK:]
-    state_out[0, 0] = hstate
-    state_out[0, 1] = gstate
-
-    search = [queries[block * BLOCK : (block + 1) * BLOCK] for block in range(blocks)]
+            grown = jnp.concatenate([keys * root_tail, values * root_tail], axis=1).astype(BF16)
+            update = dot_tn(grown, grown[:, :DK])
+            hstate = decay_last * hstate + update[:DK]
+            gstate = decay_last * gstate + update[DK:]
+        state_out[local, 0] = hstate
+        state_out[local, 1] = gstate
+
+    count = len(chains)
+    search = [chain[0] for chain in chains]
     residual = list(search)
-    solved = [None] * blocks
-    correlated = [None] * blocks
     norm_now = [jnp.sum(r * r, axis=-1, keepdims=True) for r in residual]
+    everyone = range(count)
     for iteration in range(ITERS):
-        for block in range(blocks):
-            k_high, mix_high, _, _, weights, growth = operands[block]
-            p_now = search[block]
-            p_high, p_low = halves(p_now)
-            reach = (dot_nt(p_high, k_high) + dot_nt(p_low, k_high)) * weights
-            b_high, b_low = halves(jnp.concatenate([growth * p_now, reach], axis=1))
-            applied = dot_nn(b_high, mix_high) + dot_nn(b_low, mix_high) + regular_row * p_now
-            step = norm_now[block] / jnp.sum(p_now * applied, axis=-1, keepdims=True)
-            if iteration == 0:
-                solved[block] = step * p_now
-                correlated[block] = step * reach
-            else:
-                solved[block] = solved[block] + step * p_now
-                correlated[block] = correlated[block] + step * reach
-            if iteration < ITERS - 1:
-                residual[block] = residual[block] - step * applied
-                norm_next = jnp.sum(residual[block] * residual[block], axis=-1, keepdims=True)
-                search[block] = residual[block] + norm_next / norm_now[block] * p_now
-                norm_now[block] = norm_next
+        both = [
+            dot_nn(jnp.concatenate(halves(search[index]), axis=0), chains[index][2])
+            for index in everyone
+        ]
+        both = [pair[:BLOCK] + pair[BLOCK:] for pair in both]
+        reach = [both[index][:, :BLOCK] * chains[index][5] for index in everyone]
+        near = [
+            dot_nn(jnp.concatenate(halves(reach[index]), axis=0), chains[index][1])
+            for index in everyone
+        ]
+        applied = [
+            chains[index][6] * both[index][:, BLOCK:]
+            + (near[index][:BLOCK] + near[index][BLOCK:])
+            + chains[index][7] * search[index]
+            for index in everyone
+        ]
+        step = [
+            norm_now[index] / jnp.sum(search[index] * applied[index], axis=-1, keepdims=True)
+            for index in everyone
+        ]
+        if iteration == 0:
+            solved = [step[index] * search[index] for index in everyone]
+            correlated = [step[index] * reach[index] for index in everyone]
+        else:
+            solved = [solved[index] + step[index] * search[index] for index in everyone]
+            correlated = [correlated[index] + step[index] * reach[index] for index in everyone]
+        if iteration < ITERS - 1:
+            residual = [residual[index] - step[index] * applied[index] for index in everyone]
+            norm_next = [jnp.sum(r * r, axis=-1, keepdims=True) for r in residual]
+            search = [
+                residual[index] + norm_next[index] / norm_now[index] * search[index]
+                for index in everyone
+            ]
+            norm_now = norm_next
     outputs = []
-    for block in range(blocks):
-        _, _, g_high, v_high, _, growth = operands[block]
-        recall = dot_nt((growth * solved[block]).astype(BF16), g_high)
-        outputs.append(recall + dot_nn(correlated[block].astype(BF16), v_high))
-    added = dot_nn(jnp.concatenate(outputs, axis=0).astype(BF16), out_weight[...])
-
-    @pl.when(head == 0)
+    for index in range(count):
+        _, _, _, g_high, v_high, _, growth, _ = chains[index]
+        recall = dot_nt((growth * solved[index]).astype(BF16), g_high)
+        outputs.append((recall + dot_nn(correlated[index].astype(BF16), v_high)).astype(BF16))
+    heads_out = jnp.concatenate(
+        [
+            jnp.concatenate(outputs[local * blocks : (local + 1) * blocks], axis=0)
+            for local in range(local_heads)
+        ],
+        axis=1,
+    )
+    added = dot_nn(heads_out, out_weight[...])
+    steps = pl.num_programs(0)
+
+    @pl.when(step_id == 0)
     def _():
         total[...] = added
 
-    @pl.when((head > 0) & (head < pl.num_programs(0) - 1))
+    @pl.when((step_id > 0) & (step_id < steps - 1))
     def _():
         total[...] += added
 
-    @pl.when(head == pl.num_programs(0) - 1)
+    @pl.when(step_id == steps - 1)
     def _():
         partial_out[...] = (total[...] + added).astype(BF16)
 
@@ -242,16 +270,17 @@
 def mixer(projected, taps, prefix, log_gate, regular, out_weight, length):
     rows_total = projected.shape[1]
     heads = regular.shape[0]
+    together = 2
     width = heads * DK
     features = out_weight.shape[1]
     share = prefix.shape[0] // heads
 
     def columns(part):
-        return pl.BlockSpec((1, rows_total, DK), lambda head: (part, 0, head))
+        return pl.BlockSpec((1, rows_total, together * DK), lambda step: (part, 0, step))
 
     return pl.pallas_call(
         mixer_kernel,
-        grid=(heads,),
+        grid=(heads // together,),
         out_shape=(
             jax.ShapeDtypeStruct((rows_total, features), BF16),
             jax.ShapeDtypeStruct((heads, 2, DK, DK), F32),
@@ -262,19 +291,19 @@
             columns(0),
             columns(1),
             columns(2),
-            pl.BlockSpec((3, CONV, DK), lambda head: (0, 0, head)),
-            pl.BlockSpec((share, prefix.shape[1], LANES), lambda head: (head, 0, 0)),
-            pl.BlockSpec((1, 1, rows_total), lambda head: (head, 0, 0)),
-            pl.BlockSpec((1, 1, DK), lambda head: (head, 0, 0)),
-            pl.BlockSpec((DK, features), lambda head: (head, 0)),
+            pl.BlockSpec((3, CONV, together * DK), lambda step: (0, 0, step)),
+            pl.BlockSpec((together * share, prefix.shape[1], LANES), lambda step: (step, 0, 0)),
+            pl.BlockSpec((together, 1, rows_total), lambda step: (step, 0, 0)),
+            pl.BlockSpec((together, 1, DK), lambda step: (step, 0, 0)),
+            pl.BlockSpec((together * DK, features), lambda step: (step, 0)),
         ],
         out_specs=(
-            pl.BlockSpec((rows_total, features), lambda head: (0, 0)),
-            pl.BlockSpec((1, 2, DK, DK), lambda head: (head, 0, 0, 0)),
-            pl.BlockSpec((CONV - 1, 3, 1, DK), lambda head: (0, 0, 0, head)),
+            pl.BlockSpec((rows_total, features), lambda step: (0, 0)),
+            pl.BlockSpec((together, 2, DK, DK), lambda step: (step, 0, 0, 0)),
+            pl.BlockSpec((CONV - 1, 3, 1, together * DK), lambda step: (0, 0, 0, step)),
         ),
         scratch_shapes=[
-            pltpu.VMEM((rows_total + 8, DK), F32),
+            pltpu.VMEM((together * 3, rows_total + 8, DK), F32),
             pltpu.VMEM((rows_total, features), F32),
         ],
         compiler_params=pltpu.CompilerParams(dimension_semantics=("arbitrary",)),
@@ -316,6 +345,7 @@
         request_group,
         lax.axis_size("dp"),
     )
+    packed, tokens = lax.optimization_barrier((packed, tokens))
     theirs = other_core(tokens)
     arrived = lax.all_to_all(packed, "dp", 0, 0)
     whole_rows = jnp.concatenate(

time: 68.5 us -> 64.8 us (0.946)
  Pallas kernels: 20.3 us -> 16.8 us
    pallas_call x1, Pallas kernels: 16.7 us -> 13 us  [mixer(): pl.pallas_call(mixer_kernel, grid=(heads // together,), out_shape=(jax.Sh...]
  transfers between devices with their start and end apart: 5 -> 5, of which waited for: 4 -> 4; matrix products, arithmetic and copies ran while one was open for 16% -> 16% of each run, Pallas kernels for 3% -> 0%
where the time goes in v3:
time: 64.8 us; the launch traced here: 64.4 us
  Pallas kernels  16.8 us (26%)
  waiting for transfers between devices  14.2 us (22%)
  starting transfers between devices  12.1 us (19%)
  local copies, waits for them, and re-layouts  7.61 us (12%)
  matrix products  6.48 us (10%)
  other arithmetic  4.91 us (8%)
  between operations  2.21 us (3%)
    pallas_call x1, Pallas kernels, mixer(): pl.pallas_call(mixer_kernel, grid=(heads // together,), out_shape=(jax.Sh...  13 us
    all_to_all x1, starting transfers between devices, on_device(): arrived = lax.all_to_all(packed, 'dp', 0, 0)  7.85 us
    unnamed x17, local copies, waits for them, and re-layouts  6.23 us
    all_to_all x1, waiting for transfers between devices, on_device(): prefix = lax.all_to_all(route(prefix_owner, arrived), 'dp', 0, 0)  4.79 us
    all_to_all x1, waiting for transfers between devices, on_device(): arrived = lax.all_to_all(packed, 'dp', 0, 0)  4.74 us
    ppermute x3, waiting for transfers between devices, other_core(): return lax.ppermute(array_in, 'tensor', [(0, 1), (1, 0)])  4.63 us
    dot_general x1, matrix products, on_device(): jnp.einsum('rd,jdc->jrc', normed, planes, preferred_element_type=F32)  3.56 us
    all_to_all x1, starting transfers between devices, on_device(): prefix = lax.all_to_all(route(prefix_owner, arrived), 'dp', 0, 0)  3.54 us
  transfers between devices with their start and end apart: 5, of which 4 were waited for; matrix products, arithmetic and copies ran while one was open for 16% of the time, Pallas kernels for 0%

profile of v3, /device:TPU:0, one launch (start us, length us, event | category | flops | bytes accessed | tf_op | source)
XLA Modules:
  0.0 64.4 jit_solution(11358916880815151753)
XLA Ops:
  1.4 1.9 %pack.1 = bf16[16,72,128]{2,1,0:T(8,128)(2,1)} custom-call(s32[1]{0:T(128)S(6)} %copy.19.group, f32[4,2,128,128]{3,2,1,0:T(8,128)} %bitcast.26, f32[3,3,1,512]{3,2,1,0:T(1,128)} %bitcast.28), custom_call_target="tpu_custom_call" | custom-call | tf_op jit(solution)/shard_map/pack/pallas_call | solution.py:68
  3.4 0.5 collective-permute-start
  3.9 7.9 %all-to-all-start = ((bf16[16,72,128]{2,1,0:T(8,128)(2,1)}), bf16[16,72,128]{2,1,0:T(8,128)(2,1)S(1)}, u32[]{:S(2)}, u32[]{:S(2)}) async-start(bf16[16,72,128]{2,1,0:T(8,128)(2,1)} %pack.1), calls=%async_computation | async-start | bytes 589824 | tf_op jit(solution)/shard_map/all_to_all | solution.py:350
  11.7 0.8 %fusion.26 = (f32[1,1024]{1,0:T(1,128)S(1)}, f32[1,1024]{1,0:T(1,128)S(1)}) fusion(f32[2,1024]{1,0:T(2,128)} %param.15), kind=kLoop, calls=%fused_computation.35 | loop fusion | bytes 16384 | tf_op jit(solution)/shard_map/slice | solution.py:376
  12.5 1.3 %broadcast_select_fusion.1 = (bf16[512,512]{1,0:T(8,128)(2,1)S(1)}, bf16[512,512]{1,0:T(8,128)(2,1)S(1)}) fusion(bf16[512,512]{1,0:T(8,128)(2,1)} %param.14, bf16[512,512]{1,0:T(8,128)(2,1)} %collective-permute-done, pred[]{:T(512)S(6)} %eq.3), kind=kLoop, calls=%fused_computation.29 | loop fusion | flops 524288 | bytes 2097153 | tf_op jit(solution)/shard_map/jit(_where)/select_n | solution.py:352
  13.8 0.3 fusion.5
  14.1 0.5 copy-done.1
  14.8 3.6 %fusion.9.query_in.key_in.value_in = f32[3,512,512]{2,1,0:T(8,128)} fusion(bf16[1024,3,512]{2,0,1:T(8,128)(2,1)S(1)} %copy-done, f32[1024]{0:T(1024)S(1)} %bitcast.30, f32[512]{0:T(512)S(1)} %add_rsqrt_fusion.1, bf16[512,512]{1,0:T(8,128)(2,1)S(1)} %get-tuple-element.26, bf16[512,512]{1,0:T(8,128)(2,1)S(1)} %get-tuple-element.25), kind=kOutput, calls=%fused_computation.14 | convolution fusion | flops 1614282752 | bytes 7346176 | tf_op jit(solution)/shard_map/rd,jdc->jrc/dot_general | solution.py:356
  18.4 4.7 %all-to-all-done.arrived = bf16[16,72,128]{2,1,0:T(8,128)(2,1)S(1)} async-done(((bf16[16,72,128]{2,1,0:T(8,128)(2,1)}), bf16[16,72,128]{2,1,0:T(8,128)(2,1)S(1)}, u32[]{:S(2)}, u32[]{:S(2)}) %all-to-all-start) | async-done | bytes 294944 | tf_op jit(solution)/shard_map/all_to_all | solution.py:350
  23.1 0.7 %copy-done.5 = bf16[16,72,128]{2,1,0:T(8,128)(2,1)} copy-done((bf16[16,72,128]{2,1,0:T(8,128)(2,1)}, bf16[16,72,128]{2,1,0:T(8,128)(2,1)S(1)}, u32[]{:S(2)}) %copy-start.5) | copy-done | bytes 294936
  23.8 1.9 %route.1 = bf16[16,72,128]{2,1,0:T(8,128)(2,1)} custom-call(s32[4]{0:T(128)} %owners.1, bf16[16,72,128]{2,1,0:T(8,128)(2,1)} %copy-done.5), custom_call_target="tpu_custom_call" | custom-call | tf_op jit(solution)/shard_map/route/pallas_call | solution.py:98
  25.7 3.5 %all-to-all-start.1 = ((bf16[16,72,128]{2,1,0:T(8,128)(2,1)}), bf16[16,72,128]{2,1,0:T(8,128)(2,1)S(1)}, u32[]{:S(2)}, u32[]{:S(2)}) async-start(bf16[16,72,128]{2,1,0:T(8,128)(2,1)} %route.1), calls=%async_computation.1 | async-start | bytes 589824 | tf_op jit(solution)/shard_map/all_to_all | solution.py:360
  29.9 0.6 broadcast_in_dim_squeeze.3.decay
  30.5 4.1 %copy.17 = bf16[128,8,2,768]{3,1,2,0:T(8,128)(2,1)} copy(bf16[128,8,2,768]{3,2,1,0:T(2,128)(2,1)} %bitcast.24) | data formatting | bytes 6291456
  34.6 4.8 %all-to-all-done.1.prefix = bf16[16,72,128]{2,1,0:T(8,128)(2,1)S(1)} async-done(((bf16[16,72,128]{2,1,0:T(8,128)(2,1)}), bf16[16,72,128]{2,1,0:T(8,128)(2,1)S(1)}, u32[]{:S(2)}, u32[]{:S(2)}) %all-to-all-start.1) | async-done | bytes 294944 | tf_op jit(solution)/shard_map/all_to_all | solution.py:360
  39.4 0.7 %copy-done.4 = bf16[16,72,128]{2,1,0:T(8,128)(2,1)} copy-done((bf16[16,72,128]{2,1,0:T(8,128)(2,1)}, bf16[16,72,128]{2,1,0:T(8,128)(2,1)S(1)}, u32[]{:S(2)}) %copy-start.4) | copy-done | bytes 294936
  40.1 13.0 %mixer.1 = (bf16[512,1024]{1,0:T(8,128)(2,1)}, f32[4,2,128,128]{3,2,1,0:T(8,128)}, f32[3,3,1,512]{3,2,1,0:T(1,128)}) custom-call(s32[1]{0:T(128)} %copy.18.length_ref, f32[3,512,512]{2,1,0:T(8,128)} %fusion.9.query_in.key_in.value_in, f32[3,512,512]{2,1,0:T(8,128)} %fusion.9.query_in.key_in.value_in, f32[3,512,512]{2,1,0:T(8,128)} %fusion.9.query_in.key_in.value_in, ...), custom_call_target="tpu_custom_call" | custom-call | tf_op jit(solution)/shard_map/mixer/pallas_call | solution.py:281
  53.2 2.9 %collective-permute-done.1 = bf16[512,1024]{1,0:T(8,128)(2,1)S(1)} collective-permute-done((bf16[512,1024]{1,0:T(8,128)(2,1)}, bf16[512,1024]{1,0:T(8,128)(2,1)S(1)}, u32[]{:S(2)}, u32[]{:S(2)}) %collective-permute-start.1) | collective-permute-done | bytes 1048608 | tf_op jit(solution)/shard_map/ppermute | solution.py:25
  56.1 2.1 %fusion.2 = (f32[512]{0:T(512)S(1)}, bf16[512,1024]{1,0:T(8,128)(2,1)S(1)}) fusion(bf16[512,1024]{1,0:T(8,128)(2,1)S(1)} %collective-permute-done.1, bf16[512,1024]{1,0:T(8,128)(2,1)} %get-tuple-element.19, bf16[512,512]{1,0:T(8,128)(2,1)} %copy-done.2, bf16[512,512]{1,0:T(8,128)(2,1)} %copy-done.1), kind=kLoop, calls=%fused_computation.7 | loop fusion | flops 6290944 | bytes 4196352 | tf_op jit(solution)/shard_map/reduce_sum | solution.py:20
  58.3 1.9 %fusion.15 = f32[512,1536]{1,0:T(8,128)S(1)} fusion(bf16[1024,1536]{1,0:T(8,128)(2,1)S(1)} %bitcast.25, bf16[512,1024]{1,0:T(8,128)(2,1)S(1)} %get-tuple-element.24, f32[1024]{0:T(1024)S(1)} %bitcast.29, f32[512]{0:T(512)S(1)} %add_rsqrt_fusion), kind=kOutput, calls=%fused_computation.18 | convolution fusion | flops 1612709888 | bytes 7346176 | tf_op jit(solution)/shard_map/dot_general | solution.py:375
  60.2 1.0 %fusion.21 = f32[512,1024]{1,0:T(8,128)S(1)} fusion(bf16[768,1024]{1,0:T(8,128)(2,1)S(1)} %copy-done.7, f32[512,1536]{1,0:T(8,128)S(1)} %fusion.15), kind=kOutput, calls=%fused_computation.26 | convolution fusion | flops 807665664 | bytes 6815744 | tf_op jit(solution)/shard_map/dot_general | solution.py:380
  61.3 0.2 collective-permute-start.2
  61.5 1.8 %collective-permute-done.2 = bf16[512,512]{1,0:T(8,128)(2,1)S(1)} collective-permute-done((bf16[512,512]{1,0:T(8,128)(2,1)S(1)}, bf16[512,512]{1,0:T(8,128)(2,1)S(1)}, u32[]{:S(2)}, u32[]{:S(2)}) %collective-permute-start.2) | collective-permute-done | bytes 524320 | tf_op jit(solution)/shard_map/ppermute | solution.py:25
  63.3 1.1 %select_convert_fusion = bf16[512,512]{1,0:T(8,128)(2,1)} fusion(bf16[512,512]{1,0:T(8,128)(2,1)S(1)} %collective-permute-done.2, f32[512,1024]{1,0:T(8,128)S(1)} %fusion.21, bf16[512,1024]{1,0:T(8,128)(2,1)S(1)} %get-tuple-element.24, pred[512]{0:T(512)(128)(4,1)S(1)} %iota_compare_fusion, pred[]{:T(512)S(6)} %eq.3), kind=kLoop, calls=%fused_computation.20 | loop fusion | flops 2097152 | bytes 4194817 | tf_op jit(solution)/shard_map/convert_element_type | solution.py:386
  (19 shorter events, 0.4 us)
Async XLA Ops:
  0.6 14.2 %copy-start = (bf16[1024,3,512]{2,0,1:T(8,128)(2,1)S(1)}, bf16[1024,3,512]{2,0,1:T(8,128)(2,1)}, u32[]{:S(2)}) copy-start(bf16[1024,3,512]{2,0,1:T(8,128)(2,1)} %param.16) | copy-start | bytes 9437188
  3.4 9.1 %collective-permute-start = (bf16[512,512]{1,0:T(8,128)(2,1)}, bf16[512,512]{1,0:T(8,128)(2,1)}, u32[]{:S(2)}, u32[]{:S(2)}) collective-permute-start(bf16[512,512]{1,0:T(8,128)(2,1)} %param.14), channel_id=1, source_target_pairs={{0,1},{1,0},{2,3},{3,2},{4,5},{5,4},{6,7},{7,6},{8,9},{9,8},{10,11... | collective-permute-start | bytes 1572872 | tf_op jit(solution)/shard_map/ppermute | solution.py:25
  3.9 19.2 %all-to-all-start = ((bf16[16,72,128]{2,1,0:T(8,128)(2,1)}), bf16[16,72,128]{2,1,0:T(8,128)(2,1)S(1)}, u32[]{:S(2)}, u32[]{:S(2)}) async-start(bf16[16,72,128]{2,1,0:T(8,128)(2,1)} %pack.1), calls=%async_computation | async-start | bytes 589824 | tf_op jit(solution)/shard_map/all_to_all | solution.py:350
  13.8 0.8 %copy-start.1 = (bf16[512,512]{1,0:T(8,128)(2,1)}, bf16[512,512]{1,0:T(8,128)(2,1)S(1)}, u32[]{:S(2)}) copy-start(bf16[512,512]{1,0:T(8,128)(2,1)S(1)} %get-tuple-element.25) | copy-start | bytes 1572868
  13.8 1.0 %copy-start.2 = (bf16[512,512]{1,0:T(8,128)(2,1)}, bf16[512,512]{1,0:T(8,128)(2,1)S(1)}, u32[]{:S(2)}) copy-start(bf16[512,512]{1,0:T(8,128)(2,1)S(1)} %get-tuple-element.26) | copy-start | bytes 1572868
  14.8 15.1 %copy-start.6 = (f32[1,4,512]{2,1,0:T(4,128)S(1)}, f32[1,4,512]{2,1,0:T(4,128)}, u32[]{:S(2)}) copy-start(f32[1,4,512]{2,1,0:T(4,128)} %param.18) | copy-start | bytes 24580
  23.1 0.7 %copy-start.5 = (bf16[16,72,128]{2,1,0:T(8,128)(2,1)}, bf16[16,72,128]{2,1,0:T(8,128)(2,1)S(1)}, u32[]{:S(2)}) copy-start(bf16[16,72,128]{2,1,0:T(8,128)(2,1)S(1)} %all-to-all-done.arrived) | copy-start | bytes 884740
  25.7 13.7 %all-to-all-start.1 = ((bf16[16,72,128]{2,1,0:T(8,128)(2,1)}), bf16[16,72,128]{2,1,0:T(8,128)(2,1)S(1)}, u32[]{:S(2)}, u32[]{:S(2)}) async-start(bf16[16,72,128]{2,1,0:T(8,128)(2,1)} %route.1), calls=%async_computation.1 | async-start | bytes 589824 | tf_op jit(solution)/shard_map/all_to_all | solution.py:360
  39.4 0.7 %copy-start.4 = (bf16[16,72,128]{2,1,0:T(8,128)(2,1)}, bf16[16,72,128]{2,1,0:T(8,128)(2,1)S(1)}, u32[]{:S(2)}) copy-start(bf16[16,72,128]{2,1,0:T(8,128)(2,1)S(1)} %all-to-all-done.1.prefix) | copy-start | bytes 884740
  53.1 5.1 %copy-start.3 = (bf16[128,8,2,768]{3,1,2,0:T(8,128)(2,1)S(1)}, bf16[128,8,2,768]{3,1,2,0:T(8,128)(2,1)}, u32[]{:S(2)}) copy-start(bf16[128,8,2,768]{3,1,2,0:T(8,128)(2,1)} %copy.17) | copy-start | bytes 9437188
  53.2 2.9 %collective-permute-start.1 = (bf16[512,1024]{1,0:T(8,128)(2,1)}, bf16[512,1024]{1,0:T(8,128)(2,1)S(1)}, u32[]{:S(2)}, u32[]{:S(2)}) collective-permute-start(bf16[512,1024]{1,0:T(8,128)(2,1)} %get-tuple-element.19), channel_id=1, source_target_pairs={{0,1},{1,0},{2,3},{3,2},{4,5},{5,4},{6,7},{7,6},{8,9},{9,8},{10,11... | collective-permute-start | bytes 3145736 | tf_op jit(solution)/shard_map/ppermute | solution.py:25
  58.3 1.9 %copy-start.7 = (bf16[768,1024]{1,0:T(8,128)(2,1)S(1)}, bf16[768,1024]{1,0:T(8,128)(2,1)}, u32[]{:S(2)}) copy-start(bf16[768,1024]{1,0:T(8,128)(2,1)} %param.22) | copy-start | bytes 4718596
  61.3 2.0 %collective-permute-start.2 = (bf16[512,512]{1,0:T(8,128)(2,1)S(1)}, bf16[512,512]{1,0:T(8,128)(2,1)S(1)}, u32[]{:S(2)}, u32[]{:S(2)}) collective-permute-start(bf16[512,512]{1,0:T(8,128)(2,1)S(1)} %select_convert_fusion.1), channel_id=1, source_target_pairs={{0,1},{1,0},{2,3},{3,2},{4,5},{5,4},{6,7},{7,6},{8,9},{9,8},{10,11... | collective-permute-start | bytes 1572872 | tf_op jit(solution)/shard_map/ppermute | solution.py:25

commit v4 on v3

--- a/solution.py
+++ b/solution.py
@@ -78,7 +78,8 @@
     )(request_group, prefix_cache, prefix_tail)
 
 
-def route_kernel(owners, arrived, leaving):
+def route_kernel(owners, source, target, arrived, leaving):
+    pltpu.sync_copy(source, arrived)
     count, rows, _ = arrived.shape
     groups = owners.shape[0]
     held = [arrived[owners[group]].astype(F32) for group in range(groups)]
@@ -92,43 +93,56 @@
         return carry
 
     lax.fori_loop(0, count, fill, 0)
+    pltpu.sync_copy(leaving, target)
 
 
 def route(prefix_owner, arrived):
     return pl.pallas_call(
         route_kernel,
-        out_shape=jax.ShapeDtypeStruct(arrived.shape, arrived.dtype),
+        out_shape=pltpu.HBM(arrived.shape, arrived.dtype),
         in_specs=[
             pl.BlockSpec(memory_space=pltpu.SMEM),
-            pl.BlockSpec(memory_space=pltpu.VMEM),
+            pl.BlockSpec(memory_space=pl.ANY),
         ],
-        out_specs=pl.BlockSpec(memory_space=pltpu.VMEM),
+        out_specs=pl.BlockSpec(memory_space=pltpu.HBM),
+        scratch_shapes=[pltpu.VMEM(arrived.shape, arrived.dtype)] * 2,
+        compiler_params=pltpu.CompilerParams(vmem_limit_bytes=8 << 20),
         name="route",
     )(prefix_owner, arrived)
 
 
 def mixer_kernel(
+    heads_total,
+    upper_rows,
     length_ref,
     query_in,
     key_in,
     value_in,
     taps,
-    prefix,
+    prefix_source,
     decay,
     regular,
     out_weight,
-    partial_out,
+    upper_out,
+    lower_out,
     state_out,
     tail_out,
     extended,
     total,
+    prefix,
 ):
     rows_total = query_in.shape[1]
     blocks = rows_total // BLOCK
     step_id = pl.program_id(0)
     length = length_ref[0]
     local_heads = regular.shape[0]
-    share = prefix.shape[0] // local_heads
+    steps = pl.num_programs(0)
+    share = prefix_source.shape[0] // heads_total
+
+    @pl.when(step_id == 0)
+    def _():
+        pltpu.sync_copy(prefix_source, prefix)
+
     state_rows = prefix.shape[1] - 8
     tail_rows = -(-(CONV - 1) * 3 // share)
     live = lax.broadcasted_iota(jnp.int32, (rows_total, 1), 0) < length
@@ -139,7 +153,10 @@
     chains = []
     for local in range(local_heads):
         lanes = slice(local * DK, (local + 1) * DK)
-        chunks = [prefix[local * share + piece].astype(F32) for piece in range(share)]
+        chunks = [
+            prefix[(step_id * local_heads + local) * share + piece].astype(F32)
+            for piece in range(share)
+        ]
         state = jnp.concatenate([chunk[:state_rows] for chunk in chunks], axis=0)
         hstate, gstate = state[:DK], state[DK:]
         activated = []
@@ -252,7 +269,6 @@
         axis=1,
     )
     added = dot_nn(heads_out, out_weight[...])
-    steps = pl.num_programs(0)
 
     @pl.when(step_id == 0)
     def _():
@@ -264,13 +280,17 @@
 
     @pl.when(step_id == steps - 1)
     def _():
-        partial_out[...] = (total[...] + added).astype(BF16)
+        whole = (total[...] + added).astype(BF16)
+        upper_out[...] = whole[:upper_rows]
+        lower_out[...] = whole[upper_rows:]
 
 
 def mixer(projected, taps, prefix, log_gate, regular, out_weight, length):
     rows_total = projected.shape[1]
     heads = regular.shape[0]
     together = 2
+    upper_rows = rows_total * 5 // 8
+    lower_rows = rows_total - upper_rows
     width = heads * DK
     features = out_weight.shape[1]
     share = prefix.shape[0] // heads
@@ -279,10 +299,11 @@
         return pl.BlockSpec((1, rows_total, together * DK), lambda step: (part, 0, step))
 
     return pl.pallas_call(
-        mixer_kernel,
+        functools.partial(mixer_kernel, heads, upper_rows),
         grid=(heads // together,),
         out_shape=(
-            jax.ShapeDtypeStruct((rows_total, features), BF16),
+            jax.ShapeDtypeStruct((upper_rows, features), BF16),
+            jax.ShapeDtypeStruct((lower_rows, features), BF16),
             jax.ShapeDtypeStruct((heads, 2, DK, DK), F32),
             jax.ShapeDtypeStruct((CONV - 1, 3, 1, width), F32),
         ),
@@ -292,21 +313,25 @@
             columns(1),
             columns(2),
             pl.BlockSpec((3, CONV, together * DK), lambda step: (0, 0, step)),
-            pl.BlockSpec((together * share, prefix.shape[1], LANES), lambda step: (step, 0, 0)),
+            pl.BlockSpec(memory_space=pl.ANY),
             pl.BlockSpec((together, 1, rows_total), lambda step: (step, 0, 0)),
             pl.BlockSpec((together, 1, DK), lambda step: (step, 0, 0)),
             pl.BlockSpec((together * DK, features), lambda step: (step, 0)),
         ],
         out_specs=(
-            pl.BlockSpec((rows_total, features), lambda step: (0, 0)),
+            pl.BlockSpec((upper_rows, features), lambda step: (0, 0)),
+            pl.BlockSpec((lower_rows, features), lambda step: (0, 0)),
             pl.BlockSpec((together, 2, DK, DK), lambda step: (step, 0, 0, 0)),
             pl.BlockSpec((CONV - 1, 3, 1, together * DK), lambda step: (0, 0, 0, step)),
         ),
         scratch_shapes=[
             pltpu.VMEM((together * 3, rows_total + 8, DK), F32),
             pltpu.VMEM((rows_total, features), F32),
+            pltpu.VMEM(prefix.shape, prefix.dtype),
         ],
-        compiler_params=pltpu.CompilerParams(dimension_semantics=("arbitrary",)),
+        compiler_params=pltpu.CompilerParams(
+            dimension_semantics=("arbitrary",), vmem_limit_bytes=50 << 20
+        ),
         name="mixer",
     )(
         length,
@@ -317,7 +342,7 @@
         prefix,
         log_gate[:, None, :],
         regular[:, None, :],
-        out_weight,
+        pltpu.with_memory_space_constraint(out_weight, pltpu.HBM),
     )
 
 
@@ -361,7 +386,7 @@
     prefix, gate_up_matrix = lax.optimization_barrier(
         (prefix, gate_up_weight.reshape(gate_up_weight.shape[0], -1))
     )
-    partial, state_out, tail_out = mixer(
+    upper, lower, state_out, tail_out = mixer(
         projected,
         jnp.transpose(conv_weight, (1, 0, 2)),
         prefix,
@@ -370,20 +395,29 @@
         out_weight,
         suffix_len,
     )
-    attended = partial.astype(F32) + other_core(partial).astype(F32)
-    middle = (whole_rows + attended).astype(BF16)
-    gate_up = jnp.dot(
-        rms_rows(middle.astype(F32), norm_gains[1]), gate_up_matrix, preferred_element_type=F32
-    )
-    hidden_width = gate_up.shape[1] // 2
-    hidden = (jax.nn.silu(gate_up[:, :hidden_width]) * gate_up[:, hidden_width:]).astype(BF16)
-    forward = jnp.dot(hidden, down_weight, preferred_element_type=F32)
-    left, right = forward[:, :half], forward[:, half:]
-    leaving = other_core(jnp.where(first, right, left).astype(BF16))
-    kept = jnp.where(first, left, right) + leaving.astype(F32)
-    base = jnp.where(first, middle[:, :half], middle[:, half:]).astype(F32)
-    live_rows = jnp.arange(rows_total) < suffix_len[0]
-    result = jnp.where(live_rows[:, None], base + kept, 0.0).astype(BF16)
+    hidden_width = gate_up_matrix.shape[1] // 2
+    results = []
+    for start, partial in ((0, upper), (upper.shape[0], lower)):
+        rows = slice(start, start + partial.shape[0])
+        here, there = tokens[rows], theirs[rows]
+        before = jnp.concatenate(
+            [jnp.where(first, here, there), jnp.where(first, there, here)], axis=1
+        ).astype(F32)
+        attended = partial.astype(F32) + other_core(partial).astype(F32)
+        middle = (before + attended).astype(BF16)
+        gate_up = jnp.dot(
+            rms_rows(middle.astype(F32), norm_gains[1]), gate_up_matrix, preferred_element_type=F32
+        )
+        hidden = jax.nn.silu(gate_up[:, :hidden_width]) * gate_up[:, hidden_width:]
+        forward = jnp.dot(hidden.astype(BF16), down_weight, preferred_element_type=F32)
+        left, right = forward[:, :half], forward[:, half:]
+        leaving = other_core(jnp.where(first, right, left).astype(BF16))
+        kept = jnp.where(first, left, right) + leaving.astype(F32)
+        base = jnp.where(first, middle[:, :half], middle[:, half:]).astype(F32)
+        live_rows = jnp.arange(rows.start, rows.stop) < suffix_len[0]
+        results.append(jnp.where(live_rows[:, None], base + kept, 0.0).astype(BF16))
+    result = jnp.pad(results[0], ((0, results[1].shape[0]), (0, 0)))
+    result = lax.dynamic_update_slice(result, results[1], (results[0].shape[0], 0))
     return (result, state_out[None], jnp.transpose(tail_out, (2, 0, 1, 3)))
 
 

time: 64.8 us -> 61.9 us (0.955)
  waiting for transfers between devices: 14.2 us -> 11.7 us
  local copies, waits for them, and re-layouts: 7.61 us -> 5.51 us
  starting transfers between devices: 12.1 us -> 13.2 us
  other arithmetic: 4.91 us -> 5.68 us
  Pallas kernels: 16.8 us -> 16.1 us
    ppermute x3 -> x5, waiting for transfers between devices: 4.63 us -> 1.18 us  [other_core(): return lax.ppermute(array_in, 'tensor', [(0, 1), (1, 0)])]
    select_n x0 -> x2, other arithmetic: none -> 2.13 us  [on_device(): jnp.where(first, here, there)]
    unnamed x17, local copies, waits for them, and re-layouts: 6.23 us -> 4.72 us
    reduce_sum x2 -> x3, other arithmetic: 2.42 us -> 0.97 us  [rms_rows(): jnp.mean(floats * floats, axis=-1, keepdims=True) + 1e-05]
    ppermute x3 -> x5, starting transfers between devices: 0.76 us -> 1.6 us  [other_core(): return lax.ppermute(array_in, 'tensor', [(0, 1), (1, 0)])]
    dynamic_update_slice x0 -> x1, other arithmetic: none -> 0.83 us  [on_device(): lax.dynamic_update_slice(result, results[1], (results[0].shape[0], 0))]
    convert_element_type x1 -> x2, other arithmetic: 1.09 us -> 0.34 us  [on_device(): results.append(jnp.where(live_rows[:, None], base + kept, 0.0).astype(BF16))]
    pallas_call x2, Pallas kernels: 14.9 us -> 14.2 us  [the longest x1 12.7 us: mixer(): pl.pallas_call(functools.partial(mixer_kernel, heads, upper_rows), grid=(...]
  transfers between devices with their start and end apart: 5 -> 7, of which waited for: 4 -> 3; matrix products, arithmetic and copies ran while one was open for 16% -> 27% of each run, Pallas kernels for 0% -> 0%
where the time goes in v4:
time: 61.9 us; the launch traced here: 61.4 us
  Pallas kernels  16.1 us (26%)
  starting transfers between devices  13.2 us (21%)
  waiting for transfers between devices  11.7 us (19%)
  matrix products  6.98 us (11%)
  other arithmetic  5.68 us (9%)
  local copies, waits for them, and re-layouts  5.51 us (9%)
  between operations  2.28 us (4%)
    pallas_call x1, Pallas kernels, mixer(): pl.pallas_call(functools.partial(mixer_kernel, heads, upper_rows), grid=(...  12.7 us
    all_to_all x1, starting transfers between devices, on_device(): arrived = lax.all_to_all(packed, 'dp', 0, 0)  7.85 us
    all_to_all x1, waiting for transfers between devices, on_device(): arrived = lax.all_to_all(packed, 'dp', 0, 0)  5.37 us
    all_to_all x1, waiting for transfers between devices, on_device(): prefix = lax.all_to_all(route(prefix_owner, arrived), 'dp', 0, 0)  5.14 us
    unnamed x17, local copies, waits for them, and re-layouts  4.72 us
    all_to_all x1, starting transfers between devices, on_device(): prefix = lax.all_to_all(route(prefix_owner, arrived), 'dp', 0, 0)  3.72 us
    dot_general x1, matrix products, on_device(): jnp.einsum('rd,jdc->jrc', normed, planes, preferred_element_type=F32)  3.58 us
    dot_general x2, matrix products, on_device(): jnp.dot(rms_rows(middle.astype(F32), norm_gains[1]), gate_up_matrix, pref...  2.14 us
  transfers between devices with their start and end apart: 7, of which 3 were waited for; matrix products, arithmetic and copies ran while one was open for 27% of the time, Pallas kernels for 0%

profile of v4, /device:TPU:0, one launch (start us, length us, event | category | flops | bytes accessed | tf_op | source)
XLA Modules:
  0.0 61.4 jit_solution(13602457330778402969)
XLA Ops:
  1.4 1.9 %pack.1 = bf16[16,72,128]{2,1,0:T(8,128)(2,1)} custom-call(s32[1]{0:T(128)S(6)} %copy.19.group, f32[4,2,128,128]{3,2,1,0:T(8,128)} %bitcast.32, f32[3,3,1,512]{3,2,1,0:T(1,128)} %bitcast.33), custom_call_target="tpu_custom_call" | custom-call | tf_op jit(solution)/shard_map/pack/pallas_call | solution.py:68
  3.4 0.5 collective-permute-start
  3.9 7.9 %all-to-all-start = ((bf16[16,72,128]{2,1,0:T(8,128)(2,1)}), bf16[16,72,128]{2,1,0:T(8,128)(2,1)S(1)}, u32[]{:S(2)}, u32[]{:S(2)}) async-start(bf16[16,72,128]{2,1,0:T(8,128)(2,1)} %pack.1), calls=%async_computation | async-start | bytes 589824 | tf_op jit(solution)/shard_map/all_to_all | solution.py:375
  11.7 0.8 %fusion.37 = (f32[1,1024]{1,0:T(1,128)S(1)}, f32[1,1024]{1,0:T(1,128)S(1)}) fusion(f32[2,1024]{1,0:T(2,128)} %param.15), kind=kLoop, calls=%fused_computation.59 | loop fusion | bytes 16384 | tf_op jit(solution)/shard_map/slice | solution.py:409
  12.5 1.3 %broadcast_select_fusion.1 = (bf16[512,512]{1,0:T(8,128)(2,1)S(1)}, bf16[512,512]{1,0:T(8,128)(2,1)S(1)}) fusion(bf16[512,512]{1,0:T(8,128)(2,1)} %param.14, bf16[512,512]{1,0:T(8,128)(2,1)} %collective-permute-done, pred[]{:T(512)S(6)} %eq.3), kind=kLoop, calls=%fused_computation.35 | loop fusion | flops 524288 | bytes 2097153 | tf_op jit(solution)/shard_map/jit(_where)/select_n | solution.py:377
  14.1 3.6 %fusion.5.query_in.key_in.value_in = f32[3,512,512]{2,1,0:T(8,128)} fusion(bf16[1024,3,512]{2,0,1:T(8,128)(2,1)S(1)} %copy-done, f32[1024]{0:T(1024)S(1)} %bitcast.36, f32[512]{0:T(512)S(1)} %add_rsqrt_fusion.1, bf16[512,512]{1,0:T(8,128)(2,1)S(1)} %get-tuple-element.34, bf16[512,512]{1,0:T(8,128)(2,1)S(1)} %get-tuple-element.33), kind=kOutput, calls=%fused_computation.7 | convolution fusion | flops 1614282752 | bytes 7346176 | tf_op jit(solution)/shard_map/rd,jdc->jrc/dot_general | solution.py:381
  17.7 5.4 %all-to-all-done.source = bf16[16,72,128]{2,1,0:T(8,128)(2,1)S(1)} async-done(((bf16[16,72,128]{2,1,0:T(8,128)(2,1)}), bf16[16,72,128]{2,1,0:T(8,128)(2,1)S(1)}, u32[]{:S(2)}, u32[]{:S(2)}) %all-to-all-start) | async-done | bytes 294944 | tf_op jit(solution)/shard_map/all_to_all | solution.py:375
  23.1 1.5 %route.1 = bf16[16,72,128]{2,1,0:T(8,128)(2,1)} custom-call(s32[4]{0:T(128)S(1)} %copy-done.3, bf16[16,72,128]{2,1,0:T(8,128)(2,1)S(1)} %all-to-all-done.source), custom_call_target="tpu_custom_call" | custom-call | tf_op jit(solution)/shard_map/route/pallas_call | solution.py:100
  24.6 3.7 %all-to-all-start.1 = ((bf16[16,72,128]{2,1,0:T(8,128)(2,1)}), bf16[16,72,128]{2,1,0:T(8,128)(2,1)S(1)}, u32[]{:S(2)}, u32[]{:S(2)}) async-start(bf16[16,72,128]{2,1,0:T(8,128)(2,1)} %route.1), calls=%async_computation.1 | async-start | bytes 589824 | tf_op jit(solution)/shard_map/all_to_all | solution.py:385
  29.0 4.1 %copy.17 = bf16[128,8,2,768]{3,1,2,0:T(8,128)(2,1)} copy(bf16[128,8,2,768]{3,2,1,0:T(2,128)(2,1)} %bitcast.31) | data formatting | bytes 6291456
  33.2 5.1 %all-to-all-done.1.prefix_source = bf16[16,72,128]{2,1,0:T(8,128)(2,1)S(1)} async-done(((bf16[16,72,128]{2,1,0:T(8,128)(2,1)}), bf16[16,72,128]{2,1,0:T(8,128)(2,1)S(1)}, u32[]{:S(2)}, u32[]{:S(2)}) %all-to-all-start.1) | async-done | bytes 294944 | tf_op jit(solution)/shard_map/all_to_all | solution.py:385
  38.3 12.7 %mixer.1 = (bf16[320,1024]{1,0:T(8,128)(2,1)S(1)}, bf16[192,1024]{1,0:T(8,128)(2,1)S(1)}, f32[4,2,128,128]{3,2,1,0:T(8,128)}, f32[3,3,1,512]{3,2,1,0:T(1,128)}) custom-call(s32[1]{0:T(128)} %copy.18.length_ref, f32[3,512,512]{2,1,0:T(8,128)} %fusion.5.query_in.key_in.value_in, f32[3,512,512]{2,1,0:T(8,128)} %fusion.5.query_in.key_in.value_in, ...), custom_call_target="tpu_custom_call" | custom-call | tf_op jit(solution)/shard_map/mixer/pallas_call | solution.py:301
  51.1 1.1 %broadcast_select_fusion.5 = (bf16[192,512]{1,0:T(8,128)(2,1)S(1)}, bf16[192,512]{1,0:T(8,128)(2,1)S(1)}) fusion(pred[]{:T(512)S(6)} %eq.3, bf16[512,512]{1,0:T(8,128)(2,1)} %collective-permute-done, bf16[512,512]{1,0:T(8,128)(2,1)S(1)} %copy-done.5), kind=kLoop, calls=%fused_computation.50 | loop fusion | flops 196608 | bytes 786433 | tf_op jit(solution)/shard_map/jit(_where)/select_n | solution.py:404
  52.2 1.0 %broadcast_select_fusion.3 = (bf16[320,512]{1,0:T(8,128)(2,1)S(1)}, bf16[320,512]{1,0:T(8,128)(2,1)S(1)}) fusion(pred[]{:T(512)S(6)} %eq.3, bf16[512,512]{1,0:T(8,128)(2,1)} %collective-permute-done, bf16[512,512]{1,0:T(8,128)(2,1)S(1)} %copy-done.5), kind=kLoop, calls=%fused_computation.45 | loop fusion | flops 327680 | bytes 1310721 | tf_op jit(solution)/shard_map/jit(_where)/select_n | solution.py:404
  53.2 0.4 collective-permute-start.1
  53.9 0.8 %fusion.27 = f32[192,1536]{1,0:T(8,128)S(1)} fusion(bf16[1024,1536]{1,0:T(8,128)(2,1)S(1)} %bitcast.29, bf16[192,1024]{1,0:T(8,128)(2,1)S(1)} %get-tuple-element.28, f32[1024]{0:T(1024)S(1)} %bitcast.34, f32[192]{0:T(256)S(1)} %add_rsqrt_fusion.2), kind=kOutput, calls=%fused_computation.38 | convolution fusion | flops 604766208 | bytes 4723456 | tf_op jit(solution)/shard_map/dot_general | solution.py:408
  54.8 0.5 copy-done.7
  55.3 0.5 fusion.31
  56.2 0.4 fusion.8
  56.6 1.3 %fusion.19 = f32[320,1536]{1,0:T(8,128)S(1)} fusion(bf16[1024,1536]{1,0:T(8,128)(2,1)S(1)} %bitcast.30, bf16[320,1024]{1,0:T(8,128)(2,1)S(1)} %get-tuple-element.26, f32[1024]{0:T(1024)S(1)} %bitcast.35, f32[320]{0:T(512)S(1)} %add_rsqrt_fusion), kind=kOutput, calls=%fused_computation.26 | convolution fusion | flops 1007943680 | bytes 5772544 | tf_op jit(solution)/shard_map/dot_general | solution.py:408
  57.9 0.7 %fusion.24 = f32[320,1024]{1,0:T(8,128)S(1)} fusion(bf16[768,1024]{1,0:T(8,128)(2,1)S(1)} %copy-done.7, f32[320,1536]{1,0:T(8,128)S(1)} %fusion.19), kind=kOutput, calls=%fused_computation.36 | convolution fusion | flops 504791040 | bytes 4849664 | tf_op jit(solution)/shard_map/dot_general | solution.py:412
  58.7 0.4 collective-permute-start.2
  59.2 1.2 %collective-permute-done.2 = bf16[320,512]{1,0:T(8,128)(2,1)S(1)} collective-permute-done((bf16[320,512]{1,0:T(8,128)(2,1)S(1)}, bf16[320,512]{1,0:T(8,128)(2,1)S(1)}, u32[]{:S(2)}, u32[]{:S(2)}) %collective-permute-start.2) | collective-permute-done | bytes 327712 | tf_op jit(solution)/shard_map/ppermute | solution.py:25
  60.6 0.8 %pad_maximum_fusion.2 = bf16[512,512]{1,0:T(8,128)(2,1)} fusion(bf16[192,512]{1,0:T(8,128)(2,1)S(1)} %select_convert_fusion.2, bf16[320,512]{1,0:T(8,128)(2,1)S(1)} %select_convert_fusion), kind=kLoop, calls=%fused_computation.33 | loop fusion | flops 1048576 | bytes 1048576 | tf_op jit(solution)/shard_map/dynamic_update_slice | solution.py:420
  (33 shorter events, 1.4 us)
Async XLA Ops:
  0.6 13.5 %copy-start = (bf16[1024,3,512]{2,0,1:T(8,128)(2,1)S(1)}, bf16[1024,3,512]{2,0,1:T(8,128)(2,1)}, u32[]{:S(2)}) copy-start(bf16[1024,3,512]{2,0,1:T(8,128)(2,1)} %param.16) | copy-start | bytes 9437188
  3.4 9.1 %collective-permute-start = (bf16[512,512]{1,0:T(8,128)(2,1)}, bf16[512,512]{1,0:T(8,128)(2,1)}, u32[]{:S(2)}, u32[]{:S(2)}) collective-permute-start(bf16[512,512]{1,0:T(8,128)(2,1)} %param.14), channel_id=1, source_target_pairs={{0,1},{1,0},{2,3},{3,2},{4,5},{5,4},{6,7},{7,6},{8,9},{9,8},{10,11... | collective-permute-start | bytes 1572872 | tf_op jit(solution)/shard_map/ppermute | solution.py:25
  3.9 19.2 %all-to-all-start = ((bf16[16,72,128]{2,1,0:T(8,128)(2,1)}), bf16[16,72,128]{2,1,0:T(8,128)(2,1)S(1)}, u32[]{:S(2)}, u32[]{:S(2)}) async-start(bf16[16,72,128]{2,1,0:T(8,128)(2,1)} %pack.1), calls=%async_computation | async-start | bytes 589824 | tf_op jit(solution)/shard_map/all_to_all | solution.py:375
  14.1 9.0 %copy-start.3 = (s32[4]{0:T(128)S(1)}, s32[4]{0:T(128)}, u32[]{:S(2)}) copy-start(s32[4]{0:T(128)} %owners.1) | copy-start | bytes 52
  14.1 14.8 %copy-start.6 = (f32[1,4,512]{2,1,0:T(4,128)S(1)}, f32[1,4,512]{2,1,0:T(4,128)}, u32[]{:S(2)}) copy-start(f32[1,4,512]{2,1,0:T(4,128)} %param.18) | copy-start | bytes 24580
  24.6 13.7 %all-to-all-start.1 = ((bf16[16,72,128]{2,1,0:T(8,128)(2,1)}), bf16[16,72,128]{2,1,0:T(8,128)(2,1)S(1)}, u32[]{:S(2)}, u32[]{:S(2)}) async-start(bf16[16,72,128]{2,1,0:T(8,128)(2,1)} %route.1), calls=%async_computation.1 | async-start | bytes 589824 | tf_op jit(solution)/shard_map/all_to_all | solution.py:385
  29.0 9.3 %copy-start.1 = (f32[4,3,512]{2,0,1:T(4,128)S(1)}, f32[4,3,512]{2,0,1:T(4,128)}, u32[]{:S(2)}) copy-start(f32[4,3,512]{2,0,1:T(4,128)} %param.17) | copy-start | bytes 73732
  29.0 9.3 %copy-start.2 = (f32[4,128]{1,0:T(4,128)S(1)}, f32[4,128]{1,0:T(4,128)}, u32[]{:S(2)}) copy-start(f32[4,128]{1,0:T(4,128)} %param.19) | copy-start | bytes 6148
  38.3 12.8 %copy-start.5 = (bf16[512,512]{1,0:T(8,128)(2,1)S(1)}, bf16[512,512]{1,0:T(8,128)(2,1)}, u32[]{:S(2)}) copy-start(bf16[512,512]{1,0:T(8,128)(2,1)} %param.14) | copy-start | bytes 1572868
  51.0 2.9 %copy-start.4 = (bf16[128,8,2,768]{3,1,2,0:T(8,128)(2,1)S(1)}, bf16[128,8,2,768]{3,1,2,0:T(8,128)(2,1)}, u32[]{:S(2)}) copy-start(bf16[128,8,2,768]{3,1,2,0:T(8,128)(2,1)} %copy.17) | copy-start | bytes 9437188
  51.0 2.6 %collective-permute-start.3 = (bf16[192,1024]{1,0:T(8,128)(2,1)S(1)}, bf16[192,1024]{1,0:T(8,128)(2,1)S(1)}, u32[]{:S(2)}, u32[]{:S(2)}) collective-permute-start(bf16[192,1024]{1,0:T(8,128)(2,1)S(1)} %get-tuple-element.22), channel_id=1, source_target_pairs={{0,1},{1,0},{2,3},{3,2},{4,5},{5,4},{6,7},{7,6},{8,9},{9,8},{10,11... | collective-permute-start | bytes 1179656 | tf_op jit(solution)/shard_map/ppermute | solution.py:25
  53.2 2.9 %collective-permute-start.1 = (bf16[320,1024]{1,0:T(8,128)(2,1)S(1)}, bf16[320,1024]{1,0:T(8,128)(2,1)S(1)}, u32[]{:S(2)}, u32[]{:S(2)}) collective-permute-start(bf16[320,1024]{1,0:T(8,128)(2,1)S(1)} %get-tuple-element.20), channel_id=1, source_target_pairs={{0,1},{1,0},{2,3},{3,2},{4,5},{5,4},{6,7},{7,6},{8,9},{9,8},{10,11... | collective-permute-start | bytes 1966088 | tf_op jit(solution)/shard_map/ppermute | solution.py:25
  53.9 1.4 %copy-start.7 = (bf16[768,1024]{1,0:T(8,128)(2,1)S(1)}, bf16[768,1024]{1,0:T(8,128)(2,1)}, u32[]{:S(2)}) copy-start(bf16[768,1024]{1,0:T(8,128)(2,1)} %param.22) | copy-start | bytes 4718596
  55.9 3.2 %collective-permute-start.4 = (bf16[192,512]{1,0:T(8,128)(2,1)S(1)}, bf16[192,512]{1,0:T(8,128)(2,1)S(1)}, u32[]{:S(2)}, u32[]{:S(2)}) collective-permute-start(bf16[192,512]{1,0:T(8,128)(2,1)S(1)} %select_convert_fusion.3), channel_id=1, source_target_pairs={{0,1},{1,0},{2,3},{3,2},{4,5},{5,4},{6,7},{7,6},{8,9},{9,8},{10,11... | collective-permute-start | bytes 589832 | tf_op jit(solution)/shard_map/ppermute | solution.py:25
  58.7 1.7 %collective-permute-start.2 = (bf16[320,512]{1,0:T(8,128)(2,1)S(1)}, bf16[320,512]{1,0:T(8,128)(2,1)S(1)}, u32[]{:S(2)}, u32[]{:S(2)}) collective-permute-start(bf16[320,512]{1,0:T(8,128)(2,1)S(1)} %select_convert_fusion.1), channel_id=1, source_target_pairs={{0,1},{1,0},{2,3},{3,2},{4,5},{5,4},{6,7},{7,6},{8,9},{9,8},{10,11... | collective-permute-start | bytes 983048 | tf_op jit(solution)/shard_map/ppermute | solution.py:25

commit v5 on v4

--- a/solution.py
+++ b/solution.py
@@ -197,11 +197,13 @@
             last = down[BLOCK - 1 : BLOCK, :]
             root_tail = jnp.exp(0.5 * (last - down))
             decay_last = jnp.exp(last)
+            keys_high = keys.astype(BF16)
+            mixing = jnp.concatenate([keys.T, hstate], axis=1).astype(BF16)
             chains.append(
                 (
                     queries[rows],
-                    keys.astype(BF16),
-                    jnp.concatenate([keys.T, hstate], axis=1).astype(BF16),
+                    jnp.concatenate([keys_high, keys_high], axis=0),
+                    jnp.concatenate([mixing, mixing], axis=0),
                     gstate.astype(BF16),
                     values.astype(BF16),
                     weights,
@@ -223,18 +225,17 @@
     everyone = range(count)
     for iteration in range(ITERS):
         both = [
-            dot_nn(jnp.concatenate(halves(search[index]), axis=0), chains[index][2])
+            dot_nn(jnp.concatenate(halves(search[index]), axis=1), chains[index][2])
             for index in everyone
         ]
-        both = [pair[:BLOCK] + pair[BLOCK:] for pair in both]
         reach = [both[index][:, :BLOCK] * chains[index][5] for index in everyone]
         near = [
-            dot_nn(jnp.concatenate(halves(reach[index]), axis=0), chains[index][1])
+            dot_nn(jnp.concatenate(halves(reach[index]), axis=1), chains[index][1])
             for index in everyone
         ]
         applied = [
             chains[index][6] * both[index][:, BLOCK:]
-            + (near[index][:BLOCK] + near[index][BLOCK:])
+            + near[index]
             + chains[index][7] * search[index]
             for index in everyone
         ]
@@ -375,12 +376,12 @@
     arrived = lax.all_to_all(packed, "dp", 0, 0)
     whole_rows = jnp.concatenate(
         [jnp.where(first, tokens, theirs), jnp.where(first, theirs, tokens)], axis=1
-    ).astype(F32)
-    normed = rms_rows(whole_rows, norm_gains[0])
+    )
+    normed = rms_rows(whole_rows.astype(F32), norm_gains[0])
     planes = jnp.transpose(qkv_weight, (1, 0, 2))
     projected = jnp.einsum("rd,jdc->jrc", normed, planes, preferred_element_type=F32)
-    arrived, projected, gate_up_weight = lax.optimization_barrier(
-        (arrived, projected, gate_up_weight)
+    arrived, projected, whole_rows, gate_up_weight = lax.optimization_barrier(
+        (arrived, projected, whole_rows, gate_up_weight)
     )
     prefix = lax.all_to_all(route(prefix_owner, arrived), "dp", 0, 0)
     prefix, gate_up_matrix = lax.optimization_barrier(
@@ -399,10 +400,7 @@
     results = []
     for start, partial in ((0, upper), (upper.shape[0], lower)):
         rows = slice(start, start + partial.shape[0])
-        here, there = tokens[rows], theirs[rows]
-        before = jnp.concatenate(
-            [jnp.where(first, here, there), jnp.where(first, there, here)], axis=1
-        ).astype(F32)
+        before = whole_rows[rows].astype(F32)
         attended = partial.astype(F32) + other_core(partial).astype(F32)
         middle = (before + attended).astype(BF16)
         gate_up = jnp.dot(

time: 61.9 us -> 59.7 us (0.964)
  Pallas kernels: 16.1 us -> 15 us
  other arithmetic: 5.68 us -> 4.7 us
    select_n x2 -> x0, other arithmetic: 2.13 us -> none  [on_device(): jnp.where(first, here, there)]
    ppermute x5, waiting for transfers between devices: 1.18 us -> 2.34 us  [other_core(): return lax.ppermute(array_in, 'tensor', [(0, 1), (1, 0)])]
    pallas_call x1, Pallas kernels: 12.7 us -> 11.5 us  [mixer(): pl.pallas_call(functools.partial(mixer_kernel, heads, upper_rows), grid=(...]
    concatenate x0 -> x1, other arithmetic: none -> 1.16 us  [on_device(): jnp.concatenate([jnp.where(first, tokens, theirs), jnp.where(first, their...]
    all_to_all x1, waiting for transfers between devices: 5.37 us -> 4.24 us  [on_device(): arrived = lax.all_to_all(packed, 'dp', 0, 0)]
  transfers between devices with their start and end apart: 7 -> 7, of which waited for: 3 -> 4; matrix products, arithmetic and copies ran while one was open for 27% -> 26% of each run, Pallas kernels for 0% -> 0%
where the time goes in v5:
time: 59.7 us; the launch traced here: 59.3 us
  Pallas kernels  15 us (25%)
  starting transfers between devices  13 us (22%)
  waiting for transfers between devices  11.9 us (20%)
  matrix products  6.95 us (12%)
  local copies, waits for them, and re-layouts  5.5 us (9%)
  other arithmetic  4.7 us (8%)
  between operations  2.24 us (4%)
    pallas_call x1, Pallas kernels, mixer(): pl.pallas_call(functools.partial(mixer_kernel, heads, upper_rows), grid=(...  11.5 us
    all_to_all x1, starting transfers between devices, on_device(): arrived = lax.all_to_all(packed, 'dp', 0, 0)  7.85 us
    all_to_all x1, waiting for transfers between devices, on_device(): prefix = lax.all_to_all(route(prefix_owner, arrived), 'dp', 0, 0)  5.34 us
    unnamed x17, local copies, waits for them, and re-layouts  4.71 us
    all_to_all x1, waiting for transfers between devices, on_device(): arrived = lax.all_to_all(packed, 'dp', 0, 0)  4.24 us
    dot_general x1, matrix products, on_device(): jnp.einsum('rd,jdc->jrc', normed, planes, preferred_element_type=F32)  3.57 us
    all_to_all x1, starting transfers between devices, on_device(): prefix = lax.all_to_all(route(prefix_owner, arrived), 'dp', 0, 0)  3.54 us
    ppermute x5, waiting for transfers between devices, other_core(): return lax.ppermute(array_in, 'tensor', [(0, 1), (1, 0)])  2.34 us
  transfers between devices with their start and end apart: 7, of which 4 were waited for; matrix products, arithmetic and copies ran while one was open for 26% of the time, Pallas kernels for 0%

profile of v5, /device:TPU:0, one launch (start us, length us, event | category | flops | bytes accessed | tf_op | source)
XLA Modules:
  0.0 59.3 jit_solution(2737266380646542722)
XLA Ops:
  1.4 1.9 %pack.1 = bf16[16,72,128]{2,1,0:T(8,128)(2,1)} custom-call(s32[1]{0:T(128)S(6)} %copy.19.group, f32[4,2,128,128]{3,2,1,0:T(8,128)} %bitcast.32, f32[3,3,1,512]{3,2,1,0:T(1,128)} %bitcast.33), custom_call_target="tpu_custom_call" | custom-call | tf_op jit(solution)/shard_map/pack/pallas_call | solution.py:68
  3.4 0.5 collective-permute-start
  3.9 7.9 %all-to-all-start = ((bf16[16,72,128]{2,1,0:T(8,128)(2,1)}), bf16[16,72,128]{2,1,0:T(8,128)(2,1)S(1)}, u32[]{:S(2)}, u32[]{:S(2)}) async-start(bf16[16,72,128]{2,1,0:T(8,128)(2,1)} %pack.1), calls=%async_computation | async-start | bytes 589824 | tf_op jit(solution)/shard_map/all_to_all | solution.py:376
  11.7 0.8 %fusion.36 = (f32[1,1024]{1,0:T(1,128)S(1)}, f32[1,1024]{1,0:T(1,128)S(1)}) fusion(f32[2,1024]{1,0:T(2,128)} %param.15), kind=kLoop, calls=%fused_computation.54 | loop fusion | bytes 16384 | tf_op jit(solution)/shard_map/slice | solution.py:407
  12.5 1.3 %broadcast_select_fusion.1 = (bf16[512,512]{1,0:T(8,128)(2,1)S(1)}, bf16[512,512]{1,0:T(8,128)(2,1)S(1)}) fusion(bf16[512,512]{1,0:T(8,128)(2,1)} %param.14, bf16[512,512]{1,0:T(8,128)(2,1)} %collective-permute-done, pred[]{:T(512)S(6)} %eq.3), kind=kLoop, calls=%fused_computation.35 | loop fusion | flops 524288 | bytes 2097153 | tf_op jit(solution)/shard_map/jit(_where)/select_n | solution.py:378
  14.1 1.2 %pad_maximum_fusion = bf16[512,1024]{1,0:T(8,128)(2,1)} fusion(bf16[512,512]{1,0:T(8,128)(2,1)S(1)} %get-tuple-element.32, bf16[512,512]{1,0:T(8,128)(2,1)S(1)} %get-tuple-element.31), kind=kLoop, calls=%fused_computation.15 | loop fusion | flops 2097152 | bytes 2097152 | tf_op jit(solution)/shard_map/concatenate | solution.py:377
  15.3 3.6 %fusion.5.query_in.key_in.value_in = f32[3,512,512]{2,1,0:T(8,128)} fusion(bf16[1024,3,512]{2,0,1:T(8,128)(2,1)S(1)} %copy-done, f32[1024]{0:T(1024)S(1)} %bitcast.36, f32[512]{0:T(512)S(1)} %add_rsqrt_fusion.1, bf16[512,512]{1,0:T(8,128)(2,1)S(1)} %get-tuple-element.32, bf16[512,512]{1,0:T(8,128)(2,1)S(1)} %get-tuple-element.31), kind=kOutput, calls=%fused_computation.7 | convolution fusion | flops 1614282752 | bytes 7346176 | tf_op jit(solution)/shard_map/rd,jdc->jrc/dot_general | solution.py:382
  18.9 4.2 %all-to-all-done.source = bf16[16,72,128]{2,1,0:T(8,128)(2,1)S(1)} async-done(((bf16[16,72,128]{2,1,0:T(8,128)(2,1)}), bf16[16,72,128]{2,1,0:T(8,128)(2,1)S(1)}, u32[]{:S(2)}, u32[]{:S(2)}) %all-to-all-start) | async-done | bytes 294944 | tf_op jit(solution)/shard_map/all_to_all | solution.py:376
  23.1 1.5 %route.1 = bf16[16,72,128]{2,1,0:T(8,128)(2,1)} custom-call(s32[4]{0:T(128)S(1)} %copy-done.3, bf16[16,72,128]{2,1,0:T(8,128)(2,1)S(1)} %all-to-all-done.source), custom_call_target="tpu_custom_call" | custom-call | tf_op jit(solution)/shard_map/route/pallas_call | solution.py:100
  24.6 3.5 %all-to-all-start.1 = ((bf16[16,72,128]{2,1,0:T(8,128)(2,1)}), bf16[16,72,128]{2,1,0:T(8,128)(2,1)S(1)}, u32[]{:S(2)}, u32[]{:S(2)}) async-start(bf16[16,72,128]{2,1,0:T(8,128)(2,1)} %route.1), calls=%async_computation.1 | async-start | bytes 589824 | tf_op jit(solution)/shard_map/all_to_all | solution.py:386
  28.8 4.1 %copy.17 = bf16[128,8,2,768]{3,1,2,0:T(8,128)(2,1)} copy(bf16[128,8,2,768]{3,2,1,0:T(2,128)(2,1)} %bitcast.31) | data formatting | bytes 6291456
  33.0 5.3 %all-to-all-done.1.prefix_source = bf16[16,72,128]{2,1,0:T(8,128)(2,1)S(1)} async-done(((bf16[16,72,128]{2,1,0:T(8,128)(2,1)}), bf16[16,72,128]{2,1,0:T(8,128)(2,1)S(1)}, u32[]{:S(2)}, u32[]{:S(2)}) %all-to-all-start.1) | async-done | bytes 294944 | tf_op jit(solution)/shard_map/all_to_all | solution.py:386
  38.3 11.5 %mixer.1 = (bf16[320,1024]{1,0:T(8,128)(2,1)S(1)}, bf16[192,1024]{1,0:T(8,128)(2,1)S(1)}, f32[4,2,128,128]{3,2,1,0:T(8,128)}, f32[3,3,1,512]{3,2,1,0:T(1,128)}) custom-call(s32[1]{0:T(128)} %copy.18.length_ref, f32[3,512,512]{2,1,0:T(8,128)} %fusion.5.query_in.key_in.value_in, f32[3,512,512]{2,1,0:T(8,128)} %fusion.5.query_in.key_in.value_in, ...), custom_call_target="tpu_custom_call" | custom-call | tf_op jit(solution)/shard_map/mixer/pallas_call | solution.py:302
  49.9 0.5 collective-permute-start.1
  50.4 1.2 %collective-permute-done.3 = bf16[192,1024]{1,0:T(8,128)(2,1)S(1)} collective-permute-done((bf16[192,1024]{1,0:T(8,128)(2,1)S(1)}, bf16[192,1024]{1,0:T(8,128)(2,1)S(1)}, u32[]{:S(2)}, u32[]{:S(2)}) %collective-permute-start.3) | collective-permute-done | bytes 393248 | tf_op jit(solution)/shard_map/ppermute | solution.py:25
  51.9 0.8 %fusion.27 = f32[192,1536]{1,0:T(8,128)S(1)} fusion(bf16[1024,1536]{1,0:T(8,128)(2,1)S(1)} %bitcast.29, bf16[192,1024]{1,0:T(8,128)(2,1)S(1)} %get-tuple-element.30, f32[1024]{0:T(1024)S(1)} %bitcast.34, f32[192]{0:T(256)S(1)} %add_rsqrt_fusion.2), kind=kOutput, calls=%fused_computation.38 | convolution fusion | flops 604766208 | bytes 4723456 | tf_op jit(solution)/shard_map/dot_general | solution.py:406
  52.7 0.5 copy-done.7
  53.3 0.5 fusion.31
  54.1 0.4 fusion.8
  54.5 1.3 %fusion.19 = f32[320,1536]{1,0:T(8,128)S(1)} fusion(bf16[1024,1536]{1,0:T(8,128)(2,1)S(1)} %bitcast.30, bf16[320,1024]{1,0:T(8,128)(2,1)S(1)} %get-tuple-element.28, f32[1024]{0:T(1024)S(1)} %bitcast.35, f32[320]{0:T(512)S(1)} %add_rsqrt_fusion), kind=kOutput, calls=%fused_computation.26 | convolution fusion | flops 1007943680 | bytes 5772544 | tf_op jit(solution)/shard_map/dot_general | solution.py:406
  55.8 0.7 %fusion.24 = f32[320,1024]{1,0:T(8,128)S(1)} fusion(bf16[768,1024]{1,0:T(8,128)(2,1)S(1)} %copy-done.7, f32[320,1536]{1,0:T(8,128)S(1)} %fusion.19), kind=kOutput, calls=%fused_computation.36 | convolution fusion | flops 504791040 | bytes 4849664 | tf_op jit(solution)/shard_map/dot_general | solution.py:410
  56.6 0.4 collective-permute-start.2
  57.1 1.1 %collective-permute-done.2 = bf16[320,512]{1,0:T(8,128)(2,1)S(1)} collective-permute-done((bf16[320,512]{1,0:T(8,128)(2,1)S(1)}, bf16[320,512]{1,0:T(8,128)(2,1)S(1)}, u32[]{:S(2)}, u32[]{:S(2)}) %collective-permute-start.2) | collective-permute-done | bytes 327712 | tf_op jit(solution)/shard_map/ppermute | solution.py:25
  58.5 0.8 %pad_maximum_fusion.1 = bf16[512,512]{1,0:T(8,128)(2,1)} fusion(bf16[192,512]{1,0:T(8,128)(2,1)S(1)} %select_convert_fusion.2, bf16[320,512]{1,0:T(8,128)(2,1)S(1)} %select_convert_fusion), kind=kLoop, calls=%fused_computation.33 | loop fusion | flops 1048576 | bytes 1048576 | tf_op jit(solution)/shard_map/dynamic_update_slice | solution.py:418
  (32 shorter events, 1.3 us)
Async XLA Ops:
  0.6 14.6 %copy-start = (bf16[1024,3,512]{2,0,1:T(8,128)(2,1)S(1)}, bf16[1024,3,512]{2,0,1:T(8,128)(2,1)}, u32[]{:S(2)}) copy-start(bf16[1024,3,512]{2,0,1:T(8,128)(2,1)} %param.16) | copy-start | bytes 9437188
  3.4 9.1 %collective-permute-start = (bf16[512,512]{1,0:T(8,128)(2,1)}, bf16[512,512]{1,0:T(8,128)(2,1)}, u32[]{:S(2)}, u32[]{:S(2)}) collective-permute-start(bf16[512,512]{1,0:T(8,128)(2,1)} %param.14), channel_id=1, source_target_pairs={{0,1},{1,0},{2,3},{3,2},{4,5},{5,4},{6,7},{7,6},{8,9},{9,8},{10,11... | collective-permute-start | bytes 1572872 | tf_op jit(solution)/shard_map/ppermute | solution.py:25
  3.9 19.2 %all-to-all-start = ((bf16[16,72,128]{2,1,0:T(8,128)(2,1)}), bf16[16,72,128]{2,1,0:T(8,128)(2,1)S(1)}, u32[]{:S(2)}, u32[]{:S(2)}) async-start(bf16[16,72,128]{2,1,0:T(8,128)(2,1)} %pack.1), calls=%async_computation | async-start | bytes 589824 | tf_op jit(solution)/shard_map/all_to_all | solution.py:376
  15.3 7.8 %copy-start.3 = (s32[4]{0:T(128)S(1)}, s32[4]{0:T(128)}, u32[]{:S(2)}) copy-start(s32[4]{0:T(128)} %owners.1) | copy-start | bytes 52
  15.3 13.5 %copy-start.6 = (f32[1,4,512]{2,1,0:T(4,128)S(1)}, f32[1,4,512]{2,1,0:T(4,128)}, u32[]{:S(2)}) copy-start(f32[1,4,512]{2,1,0:T(4,128)} %param.18) | copy-start | bytes 24580
  24.6 13.7 %all-to-all-start.1 = ((bf16[16,72,128]{2,1,0:T(8,128)(2,1)}), bf16[16,72,128]{2,1,0:T(8,128)(2,1)S(1)}, u32[]{:S(2)}, u32[]{:S(2)}) async-start(bf16[16,72,128]{2,1,0:T(8,128)(2,1)} %route.1), calls=%async_computation.1 | async-start | bytes 589824 | tf_op jit(solution)/shard_map/all_to_all | solution.py:386
  28.8 9.5 %copy-start.1 = (f32[4,3,512]{2,0,1:T(4,128)S(1)}, f32[4,3,512]{2,0,1:T(4,128)}, u32[]{:S(2)}) copy-start(f32[4,3,512]{2,0,1:T(4,128)} %param.17) | copy-start | bytes 73732
  28.8 9.5 %copy-start.2 = (f32[4,128]{1,0:T(4,128)S(1)}, f32[4,128]{1,0:T(4,128)}, u32[]{:S(2)}) copy-start(f32[4,128]{1,0:T(4,128)} %param.19) | copy-start | bytes 6148
  38.3 13.3 %copy-start.5 = (bf16[512,1024]{1,0:T(8,128)(2,1)S(1)}, bf16[512,1024]{1,0:T(8,128)(2,1)}, u32[]{:S(2)}) copy-start(bf16[512,1024]{1,0:T(8,128)(2,1)} %pad_maximum_fusion) | copy-start | bytes 3145732
  38.3 13.5 %copy-start.4 = (bf16[128,8,2,768]{3,1,2,0:T(8,128)(2,1)S(1)}, bf16[128,8,2,768]{3,1,2,0:T(8,128)(2,1)}, u32[]{:S(2)}) copy-start(bf16[128,8,2,768]{3,1,2,0:T(8,128)(2,1)} %copy.17) | copy-start | bytes 9437188
  49.8 1.7 %collective-permute-start.3 = (bf16[192,1024]{1,0:T(8,128)(2,1)S(1)}, bf16[192,1024]{1,0:T(8,128)(2,1)S(1)}, u32[]{:S(2)}, u32[]{:S(2)}) collective-permute-start(bf16[192,1024]{1,0:T(8,128)(2,1)S(1)} %get-tuple-element.24), channel_id=1, source_target_pairs={{0,1},{1,0},{2,3},{3,2},{4,5},{5,4},{6,7},{7,6},{8,9},{9,8},{10,11... | collective-permute-start | bytes 1179656 | tf_op jit(solution)/shard_map/ppermute | solution.py:25
  49.9 4.2 %collective-permute-start.1 = (bf16[320,1024]{1,0:T(8,128)(2,1)S(1)}, bf16[320,1024]{1,0:T(8,128)(2,1)S(1)}, u32[]{:S(2)}, u32[]{:S(2)}) collective-permute-start(bf16[320,1024]{1,0:T(8,128)(2,1)S(1)} %get-tuple-element.22), channel_id=1, source_target_pairs={{0,1},{1,0},{2,3},{3,2},{4,5},{5,4},{6,7},{7,6},{8,9},{9,8},{10,11... | collective-permute-start | bytes 1966088 | tf_op jit(solution)/shard_map/ppermute | solution.py:25
  51.9 1.4 %copy-start.7 = (bf16[768,1024]{1,0:T(8,128)(2,1)S(1)}, bf16[768,1024]{1,0:T(8,128)(2,1)}, u32[]{:S(2)}) copy-start(bf16[768,1024]{1,0:T(8,128)(2,1)} %param.22) | copy-start | bytes 4718596
  53.9 3.2 %collective-permute-start.4 = (bf16[192,512]{1,0:T(8,128)(2,1)S(1)}, bf16[192,512]{1,0:T(8,128)(2,1)S(1)}, u32[]{:S(2)}, u32[]{:S(2)}) collective-permute-start(bf16[192,512]{1,0:T(8,128)(2,1)S(1)} %select_convert_fusion.3), channel_id=1, source_target_pairs={{0,1},{1,0},{2,3},{3,2},{4,5},{5,4},{6,7},{7,6},{8,9},{9,8},{10,11... | collective-permute-start | bytes 589832 | tf_op jit(solution)/shard_map/ppermute | solution.py:25
  56.6 1.7 %collective-permute-start.2 = (bf16[320,512]{1,0:T(8,128)(2,1)S(1)}, bf16[320,512]{1,0:T(8,128)(2,1)S(1)}, u32[]{:S(2)}, u32[]{:S(2)}) collective-permute-start(bf16[320,512]{1,0:T(8,128)(2,1)S(1)} %select_convert_fusion.1), channel_id=1, source_target_pairs={{0,1},{1,0},{2,3},{3,2},{4,5},{5,4},{6,7},{7,6},{8,9},{9,8},{10,11... | collective-permute-start | bytes 983048 | tf_op jit(solution)/shard_map/ppermute | solution.py:25

commit v6 on v5

--- a/solution.py
+++ b/solution.py
@@ -92,7 +92,7 @@
         leaving[slot] = chosen.astype(BF16)
         return carry
 
-    lax.fori_loop(0, count, fill, 0)
+    lax.fori_loop(0, count, fill, 0, unroll=8)
     pltpu.sync_copy(leaving, target)
 
 
@@ -414,8 +414,9 @@
         base = jnp.where(first, middle[:, :half], middle[:, half:]).astype(F32)
         live_rows = jnp.arange(rows.start, rows.stop) < suffix_len[0]
         results.append(jnp.where(live_rows[:, None], base + kept, 0.0).astype(BF16))
-    result = jnp.pad(results[0], ((0, results[1].shape[0]), (0, 0)))
-    result = lax.dynamic_update_slice(result, results[1], (results[0].shape[0], 0))
+    result = jnp.pad(results[1], ((results[0].shape[0], 0), (0, 0)))
+    result = lax.optimization_barrier(result)
+    result = lax.dynamic_update_slice(result, results[0], (0, 0))
     return (result, state_out[None], jnp.transpose(tail_out, (2, 0, 1, 3)))
 
 

time: 59.7 us -> 59.6 us (level)
  other arithmetic: 4.7 us -> 3.87 us
  local copies, waits for them, and re-layouts: 5.5 us -> 6.32 us
    unnamed x17 -> x19, local copies, waits for them, and re-layouts: 4.71 us -> 5.5 us
    dynamic_update_slice x1, other arithmetic: 0.83 us -> 0.21 us  [on_device(): result = lax.dynamic_update_slice(result, results[0], (0, 0))]
where the time goes in v6:
time: 59.6 us; the launch traced here: 59.2 us
  Pallas kernels  14.9 us (25%)
  starting transfers between devices  13 us (22%)
  waiting for transfers between devices  11.9 us (20%)
  matrix products  6.94 us (12%)
  local copies, waits for them, and re-layouts  6.32 us (11%)
  other arithmetic  3.87 us (6%)
  between operations  2.26 us (4%)
    pallas_call x1, Pallas kernels, mixer(): pl.pallas_call(functools.partial(mixer_kernel, heads, upper_rows), grid=(...  11.5 us
    all_to_all x1, starting transfers between devices, on_device(): arrived = lax.all_to_all(packed, 'dp', 0, 0)  7.85 us
    unnamed x19, local copies, waits for them, and re-layouts  5.5 us
    all_to_all x1, waiting for transfers between devices, on_device(): prefix = lax.all_to_all(route(prefix_owner, arrived), 'dp', 0, 0)  5.34 us
    all_to_all x1, waiting for transfers between devices, on_device(): arrived = lax.all_to_all(packed, 'dp', 0, 0)  4.24 us
    dot_general x1, matrix products, on_device(): jnp.einsum('rd,jdc->jrc', normed, planes, preferred_element_type=F32)  3.57 us
    all_to_all x1, starting transfers between devices, on_device(): prefix = lax.all_to_all(route(prefix_owner, arrived), 'dp', 0, 0)  3.54 us
    ppermute x5, waiting for transfers between devices, other_core(): return lax.ppermute(array_in, 'tensor', [(0, 1), (1, 0)])  2.29 us
  transfers between devices with their start and end apart: 7, of which 4 were waited for; matrix products, arithmetic and copies ran while one was open for 26% of the time, Pallas kernels for 0%

profile of v6, /device:TPU:0, one launch (start us, length us, event | category | flops | bytes accessed | tf_op | source)
XLA Modules:
  0.0 59.2 jit_solution(18424814358232323172)
XLA Ops:
  1.4 1.9 %pack.1 = bf16[16,72,128]{2,1,0:T(8,128)(2,1)} custom-call(s32[1]{0:T(128)S(6)} %copy.20.group, f32[4,2,128,128]{3,2,1,0:T(8,128)} %bitcast.32, f32[3,3,1,512]{3,2,1,0:T(1,128)} %bitcast.33), custom_call_target="tpu_custom_call" | custom-call | tf_op jit(solution)/shard_map/pack/pallas_call | solution.py:68
  3.4 0.5 collective-permute-start
  3.9 7.9 %all-to-all-start = ((bf16[16,72,128]{2,1,0:T(8,128)(2,1)}), bf16[16,72,128]{2,1,0:T(8,128)(2,1)S(1)}, u32[]{:S(2)}, u32[]{:S(2)}) async-start(bf16[16,72,128]{2,1,0:T(8,128)(2,1)} %pack.1), calls=%async_computation | async-start | bytes 589824 | tf_op jit(solution)/shard_map/all_to_all | solution.py:376
  11.7 0.8 %fusion.37 = (f32[1,1024]{1,0:T(1,128)S(1)}, f32[1,1024]{1,0:T(1,128)S(1)}) fusion(f32[2,1024]{1,0:T(2,128)} %param.15), kind=kLoop, calls=%fused_computation.54 | loop fusion | bytes 16384 | tf_op jit(solution)/shard_map/slice | solution.py:407
  12.5 1.3 %broadcast_select_fusion.1 = (bf16[512,512]{1,0:T(8,128)(2,1)S(1)}, bf16[512,512]{1,0:T(8,128)(2,1)S(1)}) fusion(bf16[512,512]{1,0:T(8,128)(2,1)} %param.14, bf16[512,512]{1,0:T(8,128)(2,1)} %collective-permute-done, pred[]{:T(512)S(6)} %eq.3), kind=kLoop, calls=%fused_computation.34 | loop fusion | flops 524288 | bytes 2097153 | tf_op jit(solution)/shard_map/jit(_where)/select_n | solution.py:378
  14.1 1.2 %pad_maximum_fusion = bf16[512,1024]{1,0:T(8,128)(2,1)} fusion(bf16[512,512]{1,0:T(8,128)(2,1)S(1)} %get-tuple-element.32, bf16[512,512]{1,0:T(8,128)(2,1)S(1)} %get-tuple-element.31), kind=kLoop, calls=%fused_computation.15 | loop fusion | flops 2097152 | bytes 2097152 | tf_op jit(solution)/shard_map/concatenate | solution.py:377
  15.3 3.6 %fusion.5.query_in.key_in.value_in = f32[3,512,512]{2,1,0:T(8,128)} fusion(bf16[1024,3,512]{2,0,1:T(8,128)(2,1)S(1)} %copy-done, f32[1024]{0:T(1024)S(1)} %bitcast.36, f32[512]{0:T(512)S(1)} %add_rsqrt_fusion.1, bf16[512,512]{1,0:T(8,128)(2,1)S(1)} %get-tuple-element.32, bf16[512,512]{1,0:T(8,128)(2,1)S(1)} %get-tuple-element.31), kind=kOutput, calls=%fused_computation.7 | convolution fusion | flops 1614282752 | bytes 7346176 | tf_op jit(solution)/shard_map/rd,jdc->jrc/dot_general | solution.py:382
  18.9 4.2 %all-to-all-done.source = bf16[16,72,128]{2,1,0:T(8,128)(2,1)S(1)} async-done(((bf16[16,72,128]{2,1,0:T(8,128)(2,1)}), bf16[16,72,128]{2,1,0:T(8,128)(2,1)S(1)}, u32[]{:S(2)}, u32[]{:S(2)}) %all-to-all-start) | async-done | bytes 294944 | tf_op jit(solution)/shard_map/all_to_all | solution.py:376
  23.1 1.4 %route.1 = bf16[16,72,128]{2,1,0:T(8,128)(2,1)} custom-call(s32[4]{0:T(128)S(1)} %copy-done.3, bf16[16,72,128]{2,1,0:T(8,128)(2,1)S(1)} %all-to-all-done.source), custom_call_target="tpu_custom_call" | custom-call | tf_op jit(solution)/shard_map/route/pallas_call | solution.py:100
  24.5 3.5 %all-to-all-start.1 = ((bf16[16,72,128]{2,1,0:T(8,128)(2,1)}), bf16[16,72,128]{2,1,0:T(8,128)(2,1)S(1)}, u32[]{:S(2)}, u32[]{:S(2)}) async-start(bf16[16,72,128]{2,1,0:T(8,128)(2,1)} %route.1), calls=%async_computation.1 | async-start | bytes 589824 | tf_op jit(solution)/shard_map/all_to_all | solution.py:386
  28.8 4.1 %copy.17 = bf16[128,8,2,768]{3,1,2,0:T(8,128)(2,1)} copy(bf16[128,8,2,768]{3,2,1,0:T(2,128)(2,1)} %bitcast.31) | data formatting | bytes 6291456
  32.9 5.3 %all-to-all-done.1.prefix_source = bf16[16,72,128]{2,1,0:T(8,128)(2,1)S(1)} async-done(((bf16[16,72,128]{2,1,0:T(8,128)(2,1)}), bf16[16,72,128]{2,1,0:T(8,128)(2,1)S(1)}, u32[]{:S(2)}, u32[]{:S(2)}) %all-to-all-start.1) | async-done | bytes 294944 | tf_op jit(solution)/shard_map/all_to_all | solution.py:386
  38.2 11.5 %mixer.1 = (bf16[320,1024]{1,0:T(8,128)(2,1)S(1)}, bf16[192,1024]{1,0:T(8,128)(2,1)S(1)}, f32[4,2,128,128]{3,2,1,0:T(8,128)}, f32[3,3,1,512]{3,2,1,0:T(1,128)}) custom-call(s32[1]{0:T(128)} %copy.19.length_ref, f32[3,512,512]{2,1,0:T(8,128)} %fusion.5.query_in.key_in.value_in, f32[3,512,512]{2,1,0:T(8,128)} %fusion.5.query_in.key_in.value_in, ...), custom_call_target="tpu_custom_call" | custom-call | tf_op jit(solution)/shard_map/mixer/pallas_call | solution.py:302
  49.8 0.5 collective-permute-start.3
  50.3 1.2 %collective-permute-done.1 = bf16[192,1024]{1,0:T(8,128)(2,1)S(1)} collective-permute-done((bf16[192,1024]{1,0:T(8,128)(2,1)S(1)}, bf16[192,1024]{1,0:T(8,128)(2,1)S(1)}, u32[]{:S(2)}, u32[]{:S(2)}) %collective-permute-start.1) | collective-permute-done | bytes 393248 | tf_op jit(solution)/shard_map/ppermute | solution.py:25
  51.8 0.8 %fusion.27 = f32[192,1536]{1,0:T(8,128)S(1)} fusion(bf16[1024,1536]{1,0:T(8,128)(2,1)S(1)} %bitcast.29, bf16[192,1024]{1,0:T(8,128)(2,1)S(1)} %get-tuple-element.30, f32[1024]{0:T(1024)S(1)} %bitcast.34, f32[192]{0:T(256)S(1)} %add_rsqrt_fusion.2), kind=kOutput, calls=%fused_computation.37 | convolution fusion | flops 604766208 | bytes 4723456 | tf_op jit(solution)/shard_map/dot_general | solution.py:406
  52.6 0.6 copy-done.8
  53.2 0.5 fusion.32
  54.0 0.4 fusion.8
  54.4 1.3 %fusion.19 = f32[320,1536]{1,0:T(8,128)S(1)} fusion(bf16[1024,1536]{1,0:T(8,128)(2,1)S(1)} %bitcast.30, bf16[320,1024]{1,0:T(8,128)(2,1)S(1)} %get-tuple-element.28, f32[1024]{0:T(1024)S(1)} %bitcast.35, f32[320]{0:T(512)S(1)} %add_rsqrt_fusion), kind=kOutput, calls=%fused_computation.26 | convolution fusion | flops 1007943680 | bytes 5772544 | tf_op jit(solution)/shard_map/dot_general | solution.py:406
  55.7 0.7 %fusion.24 = f32[320,1024]{1,0:T(8,128)S(1)} fusion(bf16[768,1024]{1,0:T(8,128)(2,1)S(1)} %copy-done.8, f32[320,1536]{1,0:T(8,128)S(1)} %fusion.19), kind=kOutput, calls=%fused_computation.35 | convolution fusion | flops 504791040 | bytes 4849664 | tf_op jit(solution)/shard_map/dot_general | solution.py:410
  56.5 0.4 collective-permute-start.4
  57.1 1.1 %collective-permute-done.4 = bf16[320,512]{1,0:T(8,128)(2,1)S(1)} collective-permute-done((bf16[320,512]{1,0:T(8,128)(2,1)S(1)}, bf16[320,512]{1,0:T(8,128)(2,1)S(1)}, u32[]{:S(2)}, u32[]{:S(2)}) %collective-permute-start.4) | collective-permute-done | bytes 327712 | tf_op jit(solution)/shard_map/ppermute | solution.py:25
  58.4 0.8 %copy-done.6 = bf16[512,512]{1,0:T(8,128)(2,1)} copy-done((bf16[512,512]{1,0:T(8,128)(2,1)}, bf16[512,512]{1,0:T(8,128)(2,1)S(1)}, u32[]{:S(2)}) %copy-start.6) | copy-done | bytes 524312
  (34 shorter events, 1.3 us)
Async XLA Ops:
  0.6 14.7 %copy-start = (bf16[1024,3,512]{2,0,1:T(8,128)(2,1)S(1)}, bf16[1024,3,512]{2,0,1:T(8,128)(2,1)}, u32[]{:S(2)}) copy-start(bf16[1024,3,512]{2,0,1:T(8,128)(2,1)} %param.16) | copy-start | bytes 9437188
  3.4 9.1 %collective-permute-start = (bf16[512,512]{1,0:T(8,128)(2,1)}, bf16[512,512]{1,0:T(8,128)(2,1)}, u32[]{:S(2)}, u32[]{:S(2)}) collective-permute-start(bf16[512,512]{1,0:T(8,128)(2,1)} %param.14), channel_id=1, source_target_pairs={{0,1},{1,0},{2,3},{3,2},{4,5},{5,4},{6,7},{7,6},{8,9},{9,8},{10,11... | collective-permute-start | bytes 1572872 | tf_op jit(solution)/shard_map/ppermute | solution.py:25
  3.9 19.2 %all-to-all-start = ((bf16[16,72,128]{2,1,0:T(8,128)(2,1)}), bf16[16,72,128]{2,1,0:T(8,128)(2,1)S(1)}, u32[]{:S(2)}, u32[]{:S(2)}) async-start(bf16[16,72,128]{2,1,0:T(8,128)(2,1)} %pack.1), calls=%async_computation | async-start | bytes 589824 | tf_op jit(solution)/shard_map/all_to_all | solution.py:376
  15.3 7.8 %copy-start.3 = (s32[4]{0:T(128)S(1)}, s32[4]{0:T(128)}, u32[]{:S(2)}) copy-start(s32[4]{0:T(128)} %owners.1) | copy-start | bytes 52
  15.3 13.4 %copy-start.7 = (f32[1,4,512]{2,1,0:T(4,128)S(1)}, f32[1,4,512]{2,1,0:T(4,128)}, u32[]{:S(2)}) copy-start(f32[1,4,512]{2,1,0:T(4,128)} %param.18) | copy-start | bytes 24580
  24.5 13.7 %all-to-all-start.1 = ((bf16[16,72,128]{2,1,0:T(8,128)(2,1)}), bf16[16,72,128]{2,1,0:T(8,128)(2,1)S(1)}, u32[]{:S(2)}, u32[]{:S(2)}) async-start(bf16[16,72,128]{2,1,0:T(8,128)(2,1)} %route.1), calls=%async_computation.1 | async-start | bytes 589824 | tf_op jit(solution)/shard_map/all_to_all | solution.py:386
  28.7 9.5 %copy-start.1 = (f32[4,3,512]{2,0,1:T(4,128)S(1)}, f32[4,3,512]{2,0,1:T(4,128)}, u32[]{:S(2)}) copy-start(f32[4,3,512]{2,0,1:T(4,128)} %param.17) | copy-start | bytes 73732
  28.8 9.5 %copy-start.2 = (f32[4,128]{1,0:T(4,128)S(1)}, f32[4,128]{1,0:T(4,128)}, u32[]{:S(2)}) copy-start(f32[4,128]{1,0:T(4,128)} %param.19) | copy-start | bytes 6148
  38.2 13.3 %copy-start.5 = (bf16[512,1024]{1,0:T(8,128)(2,1)S(1)}, bf16[512,1024]{1,0:T(8,128)(2,1)}, u32[]{:S(2)}) copy-start(bf16[512,1024]{1,0:T(8,128)(2,1)} %pad_maximum_fusion) | copy-start | bytes 3145732
  38.2 13.5 %copy-start.4 = (bf16[128,8,2,768]{3,1,2,0:T(8,128)(2,1)S(1)}, bf16[128,8,2,768]{3,1,2,0:T(8,128)(2,1)}, u32[]{:S(2)}) copy-start(bf16[128,8,2,768]{3,1,2,0:T(8,128)(2,1)} %copy.17) | copy-start | bytes 9437188
  49.8 1.7 %collective-permute-start.1 = (bf16[192,1024]{1,0:T(8,128)(2,1)S(1)}, bf16[192,1024]{1,0:T(8,128)(2,1)S(1)}, u32[]{:S(2)}, u32[]{:S(2)}) collective-permute-start(bf16[192,1024]{1,0:T(8,128)(2,1)S(1)} %get-tuple-element.22), channel_id=1, source_target_pairs={{0,1},{1,0},{2,3},{3,2},{4,5},{5,4},{6,7},{7,6},{8,9},{9,8},{10,11... | collective-permute-start | bytes 1179656 | tf_op jit(solution)/shard_map/ppermute | solution.py:25
  49.8 4.2 %collective-permute-start.3 = (bf16[320,1024]{1,0:T(8,128)(2,1)S(1)}, bf16[320,1024]{1,0:T(8,128)(2,1)S(1)}, u32[]{:S(2)}, u32[]{:S(2)}) collective-permute-start(bf16[320,1024]{1,0:T(8,128)(2,1)S(1)} %get-tuple-element.24), channel_id=1, source_target_pairs={{0,1},{1,0},{2,3},{3,2},{4,5},{5,4},{6,7},{7,6},{8,9},{9,8},{10,11... | collective-permute-start | bytes 1966088 | tf_op jit(solution)/shard_map/ppermute | solution.py:25
  51.8 1.4 %copy-start.8 = (bf16[768,1024]{1,0:T(8,128)(2,1)S(1)}, bf16[768,1024]{1,0:T(8,128)(2,1)}, u32[]{:S(2)}) copy-start(bf16[768,1024]{1,0:T(8,128)(2,1)} %param.22) | copy-start | bytes 4718596
  53.8 3.2 %collective-permute-start.2 = (bf16[192,512]{1,0:T(8,128)(2,1)S(1)}, bf16[192,512]{1,0:T(8,128)(2,1)S(1)}, u32[]{:S(2)}, u32[]{:S(2)}) collective-permute-start(bf16[192,512]{1,0:T(8,128)(2,1)S(1)} %select_convert_fusion.3), channel_id=1, source_target_pairs={{0,1},{1,0},{2,3},{3,2},{4,5},{5,4},{6,7},{7,6},{8,9},{9,8},{10,11... | collective-permute-start | bytes 589832 | tf_op jit(solution)/shard_map/ppermute | solution.py:25
  56.5 1.7 %collective-permute-start.4 = (bf16[320,512]{1,0:T(8,128)(2,1)S(1)}, bf16[320,512]{1,0:T(8,128)(2,1)S(1)}, u32[]{:S(2)}, u32[]{:S(2)}) collective-permute-start(bf16[320,512]{1,0:T(8,128)(2,1)S(1)} %select_convert_fusion.1), channel_id=1, source_target_pairs={{0,1},{1,0},{2,3},{3,2},{4,5},{5,4},{6,7},{7,6},{8,9},{9,8},{10,11... | collective-permute-start | bytes 983048 | tf_op jit(solution)/shard_map/ppermute | solution.py:25
  58.4 0.8 %copy-start.6 = (bf16[512,512]{1,0:T(8,128)(2,1)}, bf16[512,512]{1,0:T(8,128)(2,1)S(1)}, u32[]{:S(2)}) copy-start(bf16[512,512]{1,0:T(8,128)(2,1)S(1)} %fusion.31) | copy-start | bytes 1572868
